TPU v7x, 256 devices: a whole 4x4x8 slice. The times are simulated.
256 devices in a mesh: ctx: 64 (over x, z, core), ch: 4 (over y).
Axes of the slice: x: 4, y: 4, z: 8, core: 2. Of those that a mesh axis runs over, the one named last changes fastest.
Arguments:
- short_conv_input: bfloat16 [8192, 1024], P('ctx', 'ch'), may hold values from -6 to 6
- out_gate: bfloat16 [8192, 1024], P('ctx', 'ch'), may hold values from -6 to 6
- in_gate: bfloat16 [8192, 1024], P('ctx', 'ch'), may hold values from -6 to 6
- out_cotangent: bfloat16 [8192, 1024], P('ctx', 'ch'), may hold values from -6 to 6
- mr_filter: bfloat16 [128, 64], P(None, 'ch'), may hold values from -0.5 to 0.5
- residues: float32 [16, 1024], P(None, ('ch', 'ctx')), may hold values from -5 to 5
- rates: float32 [16, 1024], P(None, ('ch', 'ctx')), may hold values from 0.00012207031 to 0.03
Outputs:
- input_grad: bfloat16 [8192, 1024], P('ctx', 'ch')
- out_gate_grad: bfloat16 [8192, 1024], P('ctx', 'ch')
- in_gate_grad: bfloat16 [8192, 1024], P('ctx', 'ch')
- filter_grad: float32 [128, 64], P(None, 'ch')
- residue_grad: float32 [16, 1024], P(None, ('ch', 'ctx'))
- rate_grad: float32 [16, 1024], P(None, ('ch', 'ctx'))
All inputs are finite; a program needn't handle non-finite values.
Results may differ from a plain program's by a relative error of at most 0.013.
Values may be sent and summed in bfloat16 or wider, within the bound.
No kernel may reach another device: no remote copies, remote signals or barrier semaphores. Data moves between devices by JAX's collectives and lax.ppermute only.
A program may use at most 64 MiB of HBM per device.

v0:
```python
import math

import jax
import jax.numpy as jnp
from jax import lax
from jax.experimental import pallas as pl
from jax.experimental.pallas import tpu as pltpu
from jax.sharding import PartitionSpec as P

F32 = jnp.float32
BF16 = jnp.bfloat16
CHUNK = 128
OWN = 4
MODES = 16
LANES = 128
IN_ROWS = 3 * OWN
OUT_ROWS = 3 * OWN + 2
NT = (((1,), (1,)), ((), ()))
TN = (((0,), (0,)), ((), ()))


def dot(left, right, dims=(((1,), (0,)), ((), ()))):
    return lax.dot_general(left, right, dims, preferred_element_type=F32)


def iota(shape, axis):
    return lax.broadcasted_iota(jnp.int32, shape, axis)


def halves(value):
    high = value.astype(BF16)
    return high, (value - high.astype(F32)).astype(BF16)


def rounded(value):
    return value.astype(BF16).astype(F32)


def mirrored(value):
    square = (value.shape[1], value.shape[1])
    flip = (iota(square, 0) + iota(square, 1) == value.shape[1] - 1).astype(BF16)
    return dot(value, flip).astype(BF16)


def diagonal_sums(square):
    rolled = pltpu.roll(square, 1, 1, stride=1, stride_axis=0)
    return jnp.sum(rolled, axis=0, keepdims=True)


def causal(square):
    return iota(square, 0) + iota(square, 1) >= square[0] - 1


def own_lanes(shape, channel):
    return (iota(shape, 1) % (OWN * MODES)) // MODES == channel


def pick_own(table, count):
    total = jnp.zeros((count, LANES), F32)
    for channel in range(OWN):
        part = table[channel * count : (channel + 1) * count]
        total = total + jnp.where(own_lanes(part.shape, channel), part, 0.0)
    return total


def pack_kernel(x_ref, k_ref, q_ref, dy_ref, out_ref):
    gated = rounded(q_ref[...].astype(F32) * dy_ref[...].astype(F32))
    tiles = (x_ref.shape[1] // 8, 8, x_ref.shape[0])
    x = x_ref[...].astype(F32).T.reshape(tiles)
    k = pltpu.roll(k_ref[...].astype(F32).T.reshape(tiles), 4, 1)
    d = gated.T.reshape(tiles)
    low = iota(tiles, 1) < 4
    rows = jnp.stack([jnp.where(low, x, k), jnp.where(low, d, x), jnp.where(low, k, d)], axis=1)
    out_ref[...] = rows.reshape(out_ref.shape).astype(BF16)


def tables_kernel(rates_ref, residues_ref, filt_ref, pick_ref, fwd_ref, bwd_ref, hf_ref, hb_ref,
                  aa_ref, bb_ref, am_ref, bm_ref, g_ref, w_ref, e_ref, lanes_ref):
    def spread(ref):
        return jnp.concatenate(
            [jnp.broadcast_to(ref[:, c : c + 1], (MODES, LANES)) for c in range(OWN)], axis=0
        )

    square = (CHUNK, CHUNK)
    row, lane = iota(square, 0), iota(square, 1)
    upper = lane >= row
    rates, residues = spread(rates_ref), spread(residues_ref)
    weights = residues * jnp.sqrt(2.0 * rates / MODES)
    shape = rates.shape
    step = iota(shape, 1).astype(F32)
    diagonal = iota(shape, 0) == iota(shape, 1) % (OWN * MODES)
    lanes_ref[0:1, :] = jnp.sum(jnp.where(diagonal, rates, 0.0), axis=0, keepdims=True)
    lanes_ref[1:2, :] = jnp.sum(jnp.where(diagonal, residues, 0.0), axis=0, keepdims=True)
    lanes_ref[2:8, :] = jnp.zeros((6, LANES), F32)
    decay = jnp.exp(-rates * step)
    after = jnp.exp(-rates * (step + 1.0))
    before = jnp.exp(-rates * (CHUNK - 1.0 - step))
    e_ref[0 : OWN * MODES, :] = decay
    e_ref[OWN * MODES :, :] = decay * step

    def wide(value):
        high, low = halves(value)
        return jnp.concatenate([jnp.concatenate([high, low], axis=1)] * 2, axis=0)

    aa_ref[...] = wide(before)
    bb_ref[...] = wide(after)
    am_ref[...] = wide(before * (CHUNK - 1.0 - step))
    bm_ref[...] = wide(after * (step + 1.0))

    def tall(value):
        high, low = halves(value)
        return jnp.concatenate([high, high, low, low], axis=0)

    g_ref[...] = tall(weights * after)
    w_ref[...] = tall(weights * before)
    terms = weights * decay
    for c in range(OWN):
        filt = jnp.sum(terms[c * MODES : (c + 1) * MODES], axis=0, keepdims=True)
        band = pltpu.roll(jnp.broadcast_to(filt, square), 0, 1, stride=1, stride_axis=0)
        high, low = halves(jnp.where(upper, band, 0.0))
        hf_ref[c] = jnp.concatenate([high, low], axis=0)
        hb_ref[c] = jnp.concatenate([high, low], axis=1)
    taps = dot(pick_ref[...], filt_ref[...], NT)[0:1]
    band = pltpu.roll(jnp.broadcast_to(taps, square), 0, 1, stride=1, stride_axis=0)
    same = jnp.where(upper, band, 0.0).astype(BF16)
    last = jnp.where(upper, 0.0, band).astype(BF16)
    fwd_ref[...] = jnp.concatenate([same, last], axis=0)
    bwd_ref[...] = jnp.concatenate([same, last], axis=1)


def main_kernel(in_ref, fwd_ref, bwd_ref, hf_ref, hb_ref, aa_ref, bb_ref, g_ref, w_ref, lanes_ref,
                out_ref, u_ref, d_ref, s_ref, in32, out32):
    count = in_ref.shape[0] // IN_ROWS
    rows = OWN * count
    in32[...] = in_ref[...].astype(F32)

    def take(which):
        return jnp.concatenate(
            [in32[pl.ds(which * OWN + c, count, stride=IN_ROWS), :] for c in range(OWN)], axis=0
        )

    def put(which, value):
        for c in range(OWN):
            out32[pl.ds(which * OWN + c, count, stride=OUT_ROWS), :] = value[c * count : (c + 1) * count]

    x, k, d = take(0), take(1), take(2)
    place = iota((rows, CHUNK), 0) % count
    x_last = jnp.where(place == 0, 0.0, pltpu.roll(x, 1, 0))
    xx = jnp.concatenate([x.astype(BF16), x_last.astype(BF16)], axis=1)
    v = rounded(dot(xx, fwd_ref[...]))
    u = (k * v).astype(BF16)
    d = d.astype(BF16)
    u_ref[...] = u
    d_ref[...] = d
    uu = jnp.concatenate([u, u], axis=1)
    dd = jnp.concatenate([d, d], axis=1)
    moment_u = pick_own(dot(uu, aa_ref[...], NT), count)
    moment_d = pick_own(dot(dd, bb_ref[...], NT), count)
    at = iota((count, LANES), 0)
    rates = lanes_ref[0:1, :]
    ahead = jnp.where(at < 1, 0.0, pltpu.roll(moment_u, 1, 0))
    behind = jnp.where(at >= count - 1, 0.0, pltpu.roll(moment_d, count - 1, 0))
    by = 1
    while by < count:
        factor = jnp.exp(rates * (-float(CHUNK) * by))
        ahead = ahead + factor * jnp.where(at < by, 0.0, pltpu.roll(ahead, by, 0))
        behind = behind + factor * jnp.where(at >= count - by, 0.0, pltpu.roll(behind, count - by, 0))
        by *= 2
    s_ref[0] = ahead
    s_ref[1] = behind
    s_ref[2] = moment_d

    def states(value):
        high = rounded(value)
        both = jnp.where(iota(value.shape, 1) < LANES // 2, high, value - high)
        parts = [jnp.where(own_lanes(value.shape, c), both, 0.0) for c in range(OWN)]
        stacked = jnp.concatenate(parts, axis=0).astype(BF16)
        return jnp.concatenate([stacked, stacked], axis=1)

    z = dot(states(ahead), g_ref[...])
    du = dot(states(behind), w_ref[...])
    z_own, du_own = [], []
    for c in range(OWN):
        part = slice(c * count, (c + 1) * count)
        z_own.append(z[part] + dot(uu[part], hf_ref[c]))
        du_own.append(du[part] + dot(dd[part], hb_ref[c], NT))
    put(0, jnp.concatenate(z_own, axis=0))
    du = rounded(jnp.concatenate(du_own, axis=0))
    put(1, du * v)
    dv = rounded(du * k)
    dv_next = jnp.where(place == count - 1, 0.0, pltpu.roll(dv, rows - 1, 0))
    dv = dv.astype(BF16)
    dvv = jnp.concatenate([dv, dv_next.astype(BF16)], axis=1)
    put(2, dot(dvv, bwd_ref[...], NT))
    same = dot(dv, mirrored(xx[:, :CHUNK]), TN)
    last = dot(dv, mirrored(xx[:, CHUNK:]), TN)
    sums = diagonal_sums(jnp.where(causal((CHUNK, CHUNK)), same, last))
    high = rounded(sums)
    out32[pl.ds(3 * OWN, count, stride=OUT_ROWS), :] = jnp.broadcast_to(high, (count, CHUNK))
    out32[pl.ds(3 * OWN + 1, count, stride=OUT_ROWS), :] = jnp.broadcast_to(sums - high, (count, CHUNK))
    out_ref[...] = out32[...].astype(BF16)


def modes_kernel(scale, u_ref, d_ref, s_ref, am_ref, bm_ref, e_ref, lanes_ref, residue_ref, rate_ref):
    count = s_ref.shape[1]
    keep = causal((CHUNK, CHUNK))
    u, d = u_ref[...], d_ref[...]
    u_mirrored = mirrored(u)
    cots = []
    for c in range(OWN):
        part = slice(c * count, (c + 1) * count)
        cots.append(diagonal_sums(jnp.where(keep, dot(d[part], u_mirrored[part], TN), 0.0)))
    cots = jnp.concatenate(cots + [jnp.zeros((8 - OWN, CHUNK), F32)], axis=0)
    inner = lax.dot_general(cots, e_ref[...], NT, precision=lax.Precision.HIGHEST,
                            preferred_element_type=F32)
    inner = jnp.where((iota(inner.shape, 1) % (OWN * MODES)) // MODES == iota(inner.shape, 0), inner, 0.0)
    inner = jnp.sum(inner, axis=0, keepdims=True)
    slope_u = pick_own(dot(jnp.concatenate([u, u], axis=1), am_ref[...], NT), count)
    slope_d = pick_own(dot(jnp.concatenate([d, d], axis=1), bm_ref[...], NT), count)
    rates, residues = lanes_ref[0:1, :], lanes_ref[1:2, :]
    ahead, behind, moment_d = s_ref[0], s_ref[1], s_ref[2]
    first = jnp.sum(ahead * moment_d, axis=0, keepdims=True)
    second = jnp.sum(
        ahead * slope_d + slope_u * behind + (CHUNK * jnp.exp(-CHUNK * rates)) * (ahead * behind),
        axis=0, keepdims=True,
    )
    half = iota((1, LANES), 1) < LANES // 2
    first = first + jnp.where(half, inner, pltpu.roll(inner, LANES // 2, 1))
    second = second + jnp.where(half, pltpu.roll(inner, LANES // 2, 1), inner)
    norm = jnp.sqrt(2.0 * rates / MODES)
    results = ((residue_ref, norm * first * scale),
               (rate_ref, residues * norm * (0.5 * first - rates * second) * scale))
    diagonal = iota((OWN * MODES, LANES), 0) == iota((OWN * MODES, LANES), 1)
    for ref, value in results:
        column = jnp.sum(jnp.where(diagonal, value, 0.0), axis=1, keepdims=True)
        for c in range(OWN):
            ref[:, c : c + 1] = column[c * MODES : (c + 1) * MODES]


def unpack_kernel(scale, in_ref, dy_ref, dx_ref, dq_ref, dk_ref, filt_ref, in32, mid32, sum32):
    count = in_ref.shape[0] // OUT_ROWS
    in32[...] = in_ref[...].astype(F32)

    def take(which):
        for c in range(OWN):
            mid32[which, pl.ds(c, count, stride=OWN), :] = in32[pl.ds(which * OWN + c, count, stride=OUT_ROWS), :]
        return mid32[which].T

    dq_ref[...] = (take(0) * dy_ref[...].astype(F32)).astype(BF16)
    dk_ref[...] = take(1).astype(BF16)
    dx_ref[...] = take(2).astype(BF16)
    sum32[...] = in32[pl.ds(3 * OWN, count, stride=OUT_ROWS), :] + in32[pl.ds(3 * OWN + 1, count, stride=OUT_ROWS), :]
    groups = filt_ref.shape[1]
    share = count // groups
    total = sum32[pl.ds(0, groups, stride=share), :]
    for i in range(1, share):
        total = total + sum32[pl.ds(i, groups, stride=share), :]
    filt_ref[...] = total.T * scale


def shape(dims, kind):
    return jax.ShapeDtypeStruct(dims, kind)


def local(x, out_gate, in_gate, out_cot, mr_filter, residues, rates):
    tokens, chans = x.shape
    peers = lax.axis_size("ctx")
    groups = mr_filter.shape[1]
    scale = 1.0 / math.sqrt(tokens * peers)
    rows = OWN * peers
    square2 = (CHUNK, 2 * CHUNK)
    tall2 = (2 * CHUNK, CHUNK)

    packed = pl.pallas_call(pack_kernel, out_shape=shape((peers * IN_ROWS, CHUNK), BF16), name="pack")(
        x, in_gate, out_gate, out_cot)
    arrived = lax.all_to_all(packed.reshape(3 * peers, OWN, CHUNK), "ctx", split_axis=0, concat_axis=0, tiled=True)

    group = lax.axis_index("ctx") * groups // peers
    pick = (lax.broadcasted_iota(jnp.int32, (8, groups), 1) == group).astype(BF16)
    fwd, bwd, hf, hb, aa, bb, am, bm, g, w, e, lanes = pl.pallas_call(
        tables_kernel,
        out_shape=(
            shape(tall2, BF16), shape(square2, BF16),
            shape((OWN,) + tall2, BF16), shape((OWN,) + square2, BF16),
            shape(square2, BF16), shape(square2, BF16), shape(square2, BF16), shape(square2, BF16),
            shape(tall2, BF16), shape(tall2, BF16),
            shape((LANES, CHUNK), F32), shape((8, LANES), F32),
        ),
        name="tables",
    )(rates, residues, mr_filter, pick)

    back, u, d, states = pl.pallas_call(
        main_kernel,
        out_shape=(shape((peers * OUT_ROWS, CHUNK), BF16), shape((rows, CHUNK), BF16),
                   shape((rows, CHUNK), BF16), shape((3, peers, LANES), F32)),
        scratch_shapes=[pltpu.VMEM((peers * IN_ROWS, CHUNK), F32), pltpu.VMEM((peers * OUT_ROWS, CHUNK), F32)],
        name="mixer",
    )(arrived.reshape(peers * IN_ROWS, CHUNK), fwd, bwd, hf, hb, aa, bb, g, w, lanes)

    returned = lax.all_to_all(back.reshape(peers * OUT_ROWS // 2, 2, CHUNK), "ctx", split_axis=0, concat_axis=0, tiled=True)

    residue_grad, rate_grad = pl.pallas_call(
        lambda *refs: modes_kernel(scale, *refs),
        out_shape=(shape(residues.shape, F32), shape(rates.shape, F32)),
        name="modes",
    )(u, d, states, am, bm, e, lanes)

    input_grad, out_gate_grad, in_gate_grad, filter_grad = pl.pallas_call(
        lambda *refs: unpack_kernel(scale, *refs),
        out_shape=(shape(x.shape, BF16), shape(x.shape, BF16), shape(x.shape, BF16), shape(mr_filter.shape, F32)),
        scratch_shapes=[pltpu.VMEM((peers * OUT_ROWS, CHUNK), F32), pltpu.VMEM((3, chans, CHUNK), F32),
                        pltpu.VMEM((peers, CHUNK), F32)],
        name="unpack",
    )(returned.reshape(peers * OUT_ROWS, CHUNK), out_cot)
    return (input_grad, out_gate_grad, in_gate_grad, filter_grad, residue_grad, rate_grad)


def solution(mesh):
    return jax.shard_map(
        local,
        mesh=mesh,
        in_specs=(
            P("ctx", "ch"),
            P("ctx", "ch"),
            P("ctx", "ch"),
            P("ctx", "ch"),
            P(None, "ch"),
            P(None, ("ch", "ctx")),
            P(None, ("ch", "ctx")),
        ),
        out_specs=(
            P("ctx", "ch"),
            P("ctx", "ch"),
            P("ctx", "ch"),
            P(None, "ch"),
            P(None, ("ch", "ctx")),
            P(None, ("ch", "ctx")),
        ),
        check_vma=False,
    )
```

profile of v0, /device:TPU:1, one launch (start us, length us, event | category | flops | bytes accessed | tf_op | source)
XLA Modules:
  0.0 50.9 jit_solution(14785856689952226881)
XLA Ops:
  0.6 1.8 %pack.1 = bf16[768,128]{1,0:T(8,128)(2,1)} custom-call(bf16[128,256]{1,0:T(8,128)(2,1)} %x_ref.1, bf16[128,256]{1,0:T(8,128)(2,1)} %k_ref.1, bf16[128,256]{1,0:T(8,128)(2,1)} %q_ref.1, bf16[128,256]{1,0:T(8,128)(2,1)} %refs_1_.1), custom_call_target="tpu_custom_call" | custom-call | tf_op jit(solution)/shard_map/pack/pallas_call | solution.py:274
  2.4 13.0 %all-to-all-start = ((bf16[192,4,128]{2,1,0:T(4,128)(2,1)}), bf16[192,4,128]{2,1,0:T(4,128)(2,1)S(1)}, u32[]{:S(2)}, u32[]{:S(2)}) async-start(bf16[192,4,128]{2,1,0:T(4,128)(2,1)} %bitcast.5), calls=%async_computation | async-start | bytes 393216 | tf_op jit(solution)/shard_map/all_to_all | solution.py:276
  15.4 0.0 copy-start.4
  15.4 0.7 %copy-done.4 = f32[16,4]{0,1:T(4,128)S(1)} copy-done((f32[16,4]{0,1:T(4,128)S(1)}, f32[16,4]{0,1:T(4,128)}, u32[]{:S(2)}) %copy-start.4) | copy-done | bytes 280
  16.1 0.0 copy-start.5
  16.1 0.7 %copy.14.residues_ref = f32[16,4]{1,0:T(8,128)} copy(f32[16,4]{0,1:T(4,128)S(1)} %copy-done.4) | data formatting | bytes 512 | tf_op args[5]
  16.7 0.0 copy-done.5
  16.8 0.0 copy-start.3
  16.8 0.7 %copy.13.rates_ref = f32[16,4]{1,0:T(8,128)} copy(f32[16,4]{0,1:T(4,128)S(1)} %copy-done.5) | data formatting | bytes 512 | tf_op args[6]
  17.4 0.0 copy-done.3
  17.4 0.7 %copy.15.filt_ref = bf16[128,16]{1,0:T(8,128)(2,1)} copy(bf16[128,16]{0,1:T(8,128)(2,1)S(1)} %copy-done.3) | data formatting | bytes 8192 | tf_op args[4]
  18.2 0.6 %iota.7.pick_ref = bf16[8,16]{1,0:T(8,128)(2,1)} broadcast(bf16[16]{0:T(256)(128)(2,1)S(1)} %compare_convert_fusion), dimensions={1} | broadcast | bytes 288 | tf_op jit(solution)/shard_map/iota | solution.py:279
  18.7 2.0 %tables.1 = (bf16[256,128]{1,0:T(8,128)(2,1)}, bf16[128,256]{1,0:T(8,128)(2,1)}, bf16[4,256,128]{2,1,0:T(8,128)(2,1)}, bf16[4,128,256]{2,1,0:T(8,128)(2,1)}, bf1...) custom-call(f32[16,4]{1,0:T(8,128)} %copy.13.rates_ref, ...), custom_call_target="tpu_custom_call" | custom-call | tf_op jit(solution)/shard_map/tables/pallas_call | solution.py:280
  20.7 5.6 %all-to-all-done = bf16[192,4,128]{2,1,0:T(4,128)(2,1)S(1)} async-done(((bf16[192,4,128]{2,1,0:T(4,128)(2,1)}), bf16[192,4,128]{2,1,0:T(4,128)(2,1)S(1)}, u32[]{:S(2)}, u32[]{:S(2)}) %all-to-all-start) | async-done | bytes 196640 | tf_op jit(solution)/shard_map/all_to_all | solution.py:276
  26.3 0.0 copy-start.1
  26.3 0.7 %copy-done.1 = bf16[192,4,128]{2,1,0:T(4,128)(2,1)} copy-done((bf16[192,4,128]{2,1,0:T(4,128)(2,1)}, bf16[192,4,128]{2,1,0:T(4,128)(2,1)S(1)}, u32[]{:S(2)}) %copy-start.1) | copy-done | bytes 196632
  27.0 3.0 %mixer.1 = (bf16[896,128]{1,0:T(8,128)(2,1)}, bf16[256,128]{1,0:T(8,128)(2,1)}, bf16[256,128]{1,0:T(8,128)(2,1)}, f32[3,64,128]{2,1,0:T(8,128)}) custom-call(bf16[768,128]{1,0:T(8,128)(2,1)} %bitcast.6, bf16[256,128]{1,0:T(8,128)(2,1)} %get-tuple-element.28.fwd_ref, bf16[128,256]{1,0:T(8,128)(2,1)} %get-tuple-element.29.bwd_ref, ...), custom_call_target="tpu_custom_call" | custom-call | tf_op jit(solution)/shard_map/mixer/pallas_call | solution.py:292
  30.0 5.7 %all-to-all-start.1 = ((bf16[448,2,128]{2,1,0:T(2,128)(2,1)}), bf16[448,2,128]{2,1,0:T(2,128)(2,1)S(1)}, u32[]{:S(2)}, u32[]{:S(2)}) async-start(bf16[448,2,128]{2,1,0:T(2,128)(2,1)} %bitcast.7), calls=%async_computation.1 | async-start | bytes 458752 | tf_op jit(solution)/shard_map/all_to_all | solution.py:300
  35.7 2.5 %modes.1 = (f32[16,4]{1,0:T(8,128)}, f32[16,4]{1,0:T(8,128)}) custom-call(bf16[256,128]{1,0:T(8,128)(2,1)} %get-tuple-element.42.refs_0_, bf16[256,128]{1,0:T(8,128)(2,1)} %get-tuple-element.43.refs_1_, f32[3,64,128]{2,1,0:T(8,128)} %get-tuple-element.44.refs_2_, bf16[128,256]{1,0:T(8,128)(2,1)} %get-tuple-element.45.refs_3_, ...), custom_call_target="tpu_custom_call" | custom-call | tf_op jit(solution)/shard_map/modes/pallas_call | solution.py:302
  38.3 0.0 copy-start.2
  38.3 1.4 %copy.17 = f32[16,4]{0,1:T(4,128)} copy(f32[16,4]{1,0:T(8,128)} %get-tuple-element.54) | data formatting | bytes 512
  39.6 0.0 copy-done.2
  39.6 0.7 %copy.18 = f32[16,4]{0,1:T(4,128)} copy(f32[16,4]{1,0:T(8,128)S(1)} %copy-done.2) | data formatting | bytes 512
  40.3 6.6 %all-to-all-done.1 = bf16[448,2,128]{2,1,0:T(2,128)(2,1)S(1)} async-done(((bf16[448,2,128]{2,1,0:T(2,128)(2,1)}), bf16[448,2,128]{2,1,0:T(2,128)(2,1)S(1)}, u32[]{:S(2)}, u32[]{:S(2)}) %all-to-all-start.1) | async-done | bytes 229408 | tf_op jit(solution)/shard_map/all_to_all | solution.py:300
  46.9 0.0 copy-start
  46.9 0.7 %copy-done = bf16[448,2,128]{2,1,0:T(2,128)(2,1)} copy-done((bf16[448,2,128]{2,1,0:T(2,128)(2,1)}, bf16[448,2,128]{2,1,0:T(2,128)(2,1)S(1)}, u32[]{:S(2)}) %copy-start) | copy-done | bytes 229400
  47.6 1.8 %unpack.1 = (bf16[128,256]{1,0:T(8,128)(2,1)}, bf16[128,256]{1,0:T(8,128)(2,1)}, bf16[128,256]{1,0:T(8,128)(2,1)}, f32[128,16]{1,0:T(8,128)}) custom-call(bf16[896,128]{1,0:T(8,128)(2,1)} %bitcast.4, bf16[128,256]{1,0:T(8,128)(2,1)} %refs_1_.1), custom_call_target="tpu_custom_call" | custom-call | tf_op jit(solution)/shard_map/unpack/pallas_call | solution.py:308
  49.4 1.5 %copy.16 = f32[128,16]{0,1:T(8,128)} copy(f32[128,16]{1,0:T(8,128)} %get-tuple-element.53) | data formatting | bytes 16384
  (1 shorter events, 0.0 us)
Async XLA Ops:
  2.4 23.9 %all-to-all-start = ((bf16[192,4,128]{2,1,0:T(4,128)(2,1)}), bf16[192,4,128]{2,1,0:T(4,128)(2,1)S(1)}, u32[]{:S(2)}, u32[]{:S(2)}) async-start(bf16[192,4,128]{2,1,0:T(4,128)(2,1)} %bitcast.5), calls=%async_computation | async-start | bytes 393216 | tf_op jit(solution)/shard_map/all_to_all | solution.py:276
  15.4 0.7 %copy-start.4 = (f32[16,4]{0,1:T(4,128)S(1)}, f32[16,4]{0,1:T(4,128)}, u32[]{:S(2)}) copy-start(f32[16,4]{0,1:T(4,128)} %param.12) | copy-start | bytes 772
  16.1 0.7 %copy-start.5 = (f32[16,4]{0,1:T(4,128)S(1)}, f32[16,4]{0,1:T(4,128)}, u32[]{:S(2)}) copy-start(f32[16,4]{0,1:T(4,128)} %param.13) | copy-start | bytes 772
  16.8 0.7 %copy-start.3 = (bf16[128,16]{0,1:T(8,128)(2,1)S(1)}, bf16[128,16]{0,1:T(8,128)(2,1)}, u32[]{:S(2)}) copy-start(bf16[128,16]{0,1:T(8,128)(2,1)} %param.11) | copy-start | bytes 12292
  26.3 0.7 %copy-start.1 = (bf16[192,4,128]{2,1,0:T(4,128)(2,1)}, bf16[192,4,128]{2,1,0:T(4,128)(2,1)S(1)}, u32[]{:S(2)}) copy-start(bf16[192,4,128]{2,1,0:T(4,128)(2,1)S(1)} %all-to-all-done) | copy-start | bytes 589828
  30.0 16.8 %all-to-all-start.1 = ((bf16[448,2,128]{2,1,0:T(2,128)(2,1)}), bf16[448,2,128]{2,1,0:T(2,128)(2,1)S(1)}, u32[]{:S(2)}, u32[]{:S(2)}) async-start(bf16[448,2,128]{2,1,0:T(2,128)(2,1)} %bitcast.7), calls=%async_computation.1 | async-start | bytes 458752 | tf_op jit(solution)/shard_map/all_to_all | solution.py:300
  38.3 1.4 %copy-start.2 = (f32[16,4]{1,0:T(8,128)S(1)}, f32[16,4]{1,0:T(8,128)}, u32[]{:S(2)}) copy-start(f32[16,4]{1,0:T(8,128)} %get-tuple-element.55) | copy-start | bytes 772
  46.9 0.7 %copy-start = (bf16[448,2,128]{2,1,0:T(2,128)(2,1)}, bf16[448,2,128]{2,1,0:T(2,128)(2,1)S(1)}, u32[]{:S(2)}) copy-start(bf16[448,2,128]{2,1,0:T(2,128)(2,1)S(1)} %all-to-all-done.1) | copy-start | bytes 688132
where the time goes:
time: 51.4 us; the launch traced here: 50.9 us
  starting transfers between devices  18.7 us (36%)
  waiting for transfers between devices  12.2 us (24%)
  Pallas kernels  11.1 us (22%)
  local copies, waits for them, and re-layouts  8.22 us (16%)
  between operations  0.68 us (1%)
    all_to_all x1, starting transfers between devices, local(): lax.all_to_all(packed.reshape(3 * peers, OWN, CHUNK), 'ctx', split_axis=0...  13 us
    unnamed x18, local copies, waits for them, and re-layouts  7.64 us
    all_to_all x1, waiting for transfers between devices, local(): lax.all_to_all(back.reshape(peers * OUT_ROWS // 2, 2, CHUNK), 'ctx', spli...  6.6 us
    all_to_all x1, starting transfers between devices, local(): lax.all_to_all(back.reshape(peers * OUT_ROWS // 2, 2, CHUNK), 'ctx', spli...  5.7 us
    all_to_all x1, waiting for transfers between devices, local(): lax.all_to_all(packed.reshape(3 * peers, OWN, CHUNK), 'ctx', split_axis=0...  5.61 us
    pallas_call x1, Pallas kernels, local(): pl.pallas_call(main_kernel, out_shape=(shape((peers * OUT_ROWS, CHUNK), B...  3.05 us
    pallas_call x1, Pallas kernels, local(): pl.pallas_call(lambda *refs: modes_kernel(scale, *refs), out_shape=(shape...  2.52 us
    pallas_call x1, Pallas kernels, local(): pl.pallas_call(tables_kernel, out_shape=(shape(tall2, BF16), shape(square...  1.97 us
  transfers between devices with their start and end apart: 2, of which 2 were waited for; matrix products, arithmetic and copies ran while one was open for 9% of the time, Pallas kernels for 9%

commit v1 on v0

--- a/solution.py
+++ b/solution.py
@@ -77,8 +77,9 @@
 def tables_kernel(rates_ref, residues_ref, filt_ref, pick_ref, fwd_ref, bwd_ref, hf_ref, hb_ref,
                   aa_ref, bb_ref, am_ref, bm_ref, g_ref, w_ref, e_ref, lanes_ref):
     def spread(ref):
+        columns = ref[...].T
         return jnp.concatenate(
-            [jnp.broadcast_to(ref[:, c : c + 1], (MODES, LANES)) for c in range(OWN)], axis=0
+            [jnp.broadcast_to(columns[:, c : c + 1], (MODES, LANES)) for c in range(OWN)], axis=0
         )
 
     square = (CHUNK, CHUNK)
@@ -120,7 +121,7 @@
         high, low = halves(jnp.where(upper, band, 0.0))
         hf_ref[c] = jnp.concatenate([high, low], axis=0)
         hb_ref[c] = jnp.concatenate([high, low], axis=1)
-    taps = dot(pick_ref[...], filt_ref[...], NT)[0:1]
+    taps = dot(pick_ref[...], filt_ref[...])[0:1]
     band = pltpu.roll(jnp.broadcast_to(taps, square), 0, 1, stride=1, stride_axis=0)
     same = jnp.where(upper, band, 0.0).astype(BF16)
     last = jnp.where(upper, 0.0, band).astype(BF16)
@@ -230,11 +231,9 @@
     norm = jnp.sqrt(2.0 * rates / MODES)
     results = ((residue_ref, norm * first * scale),
                (rate_ref, residues * norm * (0.5 * first - rates * second) * scale))
-    diagonal = iota((OWN * MODES, LANES), 0) == iota((OWN * MODES, LANES), 1)
     for ref, value in results:
-        column = jnp.sum(jnp.where(diagonal, value, 0.0), axis=1, keepdims=True)
         for c in range(OWN):
-            ref[:, c : c + 1] = column[c * MODES : (c + 1) * MODES]
+            ref[c : c + 1, :] = value[:, c * MODES : (c + 1) * MODES]
 
 
 def unpack_kernel(scale, in_ref, dy_ref, dx_ref, dq_ref, dk_ref, filt_ref, in32, mid32, sum32):
@@ -250,12 +249,15 @@
     dk_ref[...] = take(1).astype(BF16)
     dx_ref[...] = take(2).astype(BF16)
     sum32[...] = in32[pl.ds(3 * OWN, count, stride=OUT_ROWS), :] + in32[pl.ds(3 * OWN + 1, count, stride=OUT_ROWS), :]
-    groups = filt_ref.shape[1]
+    groups = filt_ref.shape[0]
     share = count // groups
     total = sum32[pl.ds(0, groups, stride=share), :]
     for i in range(1, share):
         total = total + sum32[pl.ds(i, groups, stride=share), :]
-    filt_ref[...] = total.T * scale
+    filt_ref[...] = total * scale
+
+
+ROOM = pltpu.CompilerParams(vmem_limit_bytes=8 * 1024 * 1024)
 
 
 def shape(dims, kind):
@@ -286,33 +288,33 @@
             shape(tall2, BF16), shape(tall2, BF16),
             shape((LANES, CHUNK), F32), shape((8, LANES), F32),
         ),
-        name="tables",
-    )(rates, residues, mr_filter, pick)
+        compiler_params=ROOM, name="tables",
+    )(rates.T, residues.T, mr_filter.T, pick)
 
     back, u, d, states = pl.pallas_call(
         main_kernel,
         out_shape=(shape((peers * OUT_ROWS, CHUNK), BF16), shape((rows, CHUNK), BF16),
                    shape((rows, CHUNK), BF16), shape((3, peers, LANES), F32)),
         scratch_shapes=[pltpu.VMEM((peers * IN_ROWS, CHUNK), F32), pltpu.VMEM((peers * OUT_ROWS, CHUNK), F32)],
-        name="mixer",
+        compiler_params=ROOM, name="mixer",
     )(arrived.reshape(peers * IN_ROWS, CHUNK), fwd, bwd, hf, hb, aa, bb, g, w, lanes)
 
     returned = lax.all_to_all(back.reshape(peers * OUT_ROWS // 2, 2, CHUNK), "ctx", split_axis=0, concat_axis=0, tiled=True)
 
     residue_grad, rate_grad = pl.pallas_call(
         lambda *refs: modes_kernel(scale, *refs),
-        out_shape=(shape(residues.shape, F32), shape(rates.shape, F32)),
-        name="modes",
+        out_shape=(shape(residues.shape[::-1], F32), shape(rates.shape[::-1], F32)),
+        compiler_params=ROOM, name="modes",
     )(u, d, states, am, bm, e, lanes)
 
     input_grad, out_gate_grad, in_gate_grad, filter_grad = pl.pallas_call(
         lambda *refs: unpack_kernel(scale, *refs),
-        out_shape=(shape(x.shape, BF16), shape(x.shape, BF16), shape(x.shape, BF16), shape(mr_filter.shape, F32)),
+        out_shape=(shape(x.shape, BF16), shape(x.shape, BF16), shape(x.shape, BF16), shape(mr_filter.shape[::-1], F32)),
         scratch_shapes=[pltpu.VMEM((peers * OUT_ROWS, CHUNK), F32), pltpu.VMEM((3, chans, CHUNK), F32),
                         pltpu.VMEM((peers, CHUNK), F32)],
-        name="unpack",
+        compiler_params=ROOM, name="unpack",
     )(returned.reshape(peers * OUT_ROWS, CHUNK), out_cot)
-    return (input_grad, out_gate_grad, in_gate_grad, filter_grad, residue_grad, rate_grad)
+    return (input_grad, out_gate_grad, in_gate_grad, filter_grad.T, residue_grad.T, rate_grad.T)
 
 
 def solution(mesh):

time: 51.4 us -> 46.1 us (0.90)
  local copies, waits for them, and re-layouts: 8.22 us -> 0.69 us
  waiting for transfers between devices: 12.2 us -> 19.5 us
  Pallas kernels: 11.1 us -> 6.14 us
    unnamed x18 -> x8, local copies, waits for them, and re-layouts: 7.64 us -> 0.69 us
    all_to_all x1, waiting for transfers between devices: 5.61 us -> 9.87 us  [local(): lax.all_to_all(packed.reshape(3 * peers, OWN, CHUNK), 'ctx', split_axis=0...]
    all_to_all x1, waiting for transfers between devices: 6.6 us -> 9.68 us  [local(): lax.all_to_all(back.reshape(peers * OUT_ROWS // 2, 2, CHUNK), 'ctx', spli...]
    pallas_call x1, Pallas kernels: 1.97 us -> 0.32 us  [local(): pl.pallas_call(tables_kernel, out_shape=(shape(tall2, BF16), shape(square...]
    pallas_call x1, Pallas kernels: 3.05 us -> 1.8 us  [local(): pl.pallas_call(main_kernel, out_shape=(shape((peers * OUT_ROWS, CHUNK), B...]
    pallas_call x1, Pallas kernels: 2.52 us -> 1.44 us  [local(): pl.pallas_call(lambda *refs: modes_kernel(scale, *refs), out_shape=(shape...]
    pallas_call x1, Pallas kernels: 1.79 us -> 0.83 us  [local(): pl.pallas_call(lambda *refs: unpack_kernel(scale, *refs), out_shape=(shap...]
    iota x1, local copies, waits for them, and re-layouts: 0.58 us -> 0.01 us  [local(): lax.broadcasted_iota(jnp.int32, (8, groups), 1) == group]
  transfers between devices with their start and end apart: 2 -> 2, of which waited for: 2 -> 2; matrix products, arithmetic and copies ran while one was open for 9% -> 0% of each run, Pallas kernels for 9% -> 4%
where the time goes in v1:
time: 46.1 us; the launch traced here: 45.8 us
  waiting for transfers between devices  19.5 us (42%)
  starting transfers between devices  18.7 us (41%)
  Pallas kernels  6.14 us (13%)
  between operations  0.72 us (2%)
  local copies, waits for them, and re-layouts  0.69 us (1%)
    all_to_all x1, starting transfers between devices, local(): lax.all_to_all(packed.reshape(3 * peers, OWN, CHUNK), 'ctx', split_axis=0...  13 us
    all_to_all x1, waiting for transfers between devices, local(): lax.all_to_all(packed.reshape(3 * peers, OWN, CHUNK), 'ctx', split_axis=0...  9.87 us
    all_to_all x1, waiting for transfers between devices, local(): lax.all_to_all(back.reshape(peers * OUT_ROWS // 2, 2, CHUNK), 'ctx', spli...  9.68 us
    all_to_all x1, starting transfers between devices, local(): lax.all_to_all(back.reshape(peers * OUT_ROWS // 2, 2, CHUNK), 'ctx', spli...  5.7 us
    pallas_call x1, Pallas kernels, local(): pl.pallas_call(main_kernel, out_shape=(shape((peers * OUT_ROWS, CHUNK), B...  1.8 us
    pallas_call x1, Pallas kernels, local(): pl.pallas_call(pack_kernel, out_shape=shape((peers * IN_ROWS, CHUNK), BF1...  1.75 us
    pallas_call x1, Pallas kernels, local(): pl.pallas_call(lambda *refs: modes_kernel(scale, *refs), out_shape=(shape...  1.44 us
  transfers between devices with their start and end apart: 2, of which 2 were waited for; matrix products, arithmetic and copies ran while one was open for 0% of the time, Pallas kernels for 4%

profile of v1, /device:TPU:1, one launch (start us, length us, event | category | flops | bytes accessed | tf_op | source)
XLA Modules:
  0.0 45.8 jit_solution(17761668606515202503)
XLA Ops:
  0.6 1.8 %pack.1 = bf16[768,128]{1,0:T(8,128)(2,1)} custom-call(bf16[128,256]{1,0:T(8,128)(2,1)} %x_ref.1, bf16[128,256]{1,0:T(8,128)(2,1)} %k_ref.1, bf16[128,256]{1,0:T(8,128)(2,1)} %q_ref.1, bf16[128,256]{1,0:T(8,128)(2,1)} %refs_1_.1), custom_call_target="tpu_custom_call" | custom-call | tf_op jit(solution)/shard_map/pack/pallas_call | solution.py:276
  2.4 13.0 %all-to-all-start = ((bf16[192,4,128]{2,1,0:T(4,128)(2,1)}), bf16[192,4,128]{2,1,0:T(4,128)(2,1)S(1)}, u32[]{:S(2)}, u32[]{:S(2)}) async-start(bf16[192,4,128]{2,1,0:T(4,128)(2,1)} %bitcast.15), calls=%async_computation | async-start | bytes 393216 | tf_op jit(solution)/shard_map/all_to_all | solution.py:278
  15.4 0.0 copy-start.1
  15.4 0.0 copy-start.2
  15.4 0.0 copy-start.3
  15.5 0.6 %copy-done.1 = bf16[128,16]{0,1:T(8,128)(2,1)S(1)} copy-done((bf16[128,16]{0,1:T(8,128)(2,1)S(1)}, bf16[128,16]{0,1:T(8,128)(2,1)}, u32[]{:S(2)}) %copy-start.1) | copy-done | bytes 4120
  16.1 0.0 copy-done.2
  16.1 0.0 copy-done.3
  16.1 0.3 tables.1
  16.4 9.9 %all-to-all-done = bf16[192,4,128]{2,1,0:T(4,128)(2,1)S(1)} async-done(((bf16[192,4,128]{2,1,0:T(4,128)(2,1)}), bf16[192,4,128]{2,1,0:T(4,128)(2,1)S(1)}, u32[]{:S(2)}, u32[]{:S(2)}) %all-to-all-start) | async-done | bytes 196640 | tf_op jit(solution)/shard_map/all_to_all | solution.py:278
  26.3 1.8 %mixer.1 = (bf16[896,128]{1,0:T(8,128)(2,1)}, bf16[256,128]{1,0:T(8,128)(2,1)S(1)}, bf16[256,128]{1,0:T(8,128)(2,1)S(1)}, f32[3,64,128]{2,1,0:T(8,128)S(1)}) custom-call(bf16[768,128]{1,0:T(8,128)(2,1)S(1)} %bitcast.11, bf16[256,128]{1,0:T(8,128)(2,1)S(1)} %get-tuple-element.28.fwd_ref, bf16[128,256]{1,0:T(8,128)(2,1)S(1)} %get-tuple-element.29.bwd_ref, ...), custom_call_target="tpu_custom_call" | custom-call | tf_op jit(solution)/shard_map/mixer/pallas_call | solution.py:294
  28.1 5.7 %all-to-all-start.1 = ((bf16[448,2,128]{2,1,0:T(2,128)(2,1)}), bf16[448,2,128]{2,1,0:T(2,128)(2,1)S(1)}, u32[]{:S(2)}, u32[]{:S(2)}) async-start(bf16[448,2,128]{2,1,0:T(2,128)(2,1)} %bitcast.5), calls=%async_computation.1 | async-start | bytes 458752 | tf_op jit(solution)/shard_map/all_to_all | solution.py:302
  33.8 0.0 copy-start
  33.8 1.4 %modes.1 = (f32[4,16]{1,0:T(4,128)}, f32[4,16]{1,0:T(4,128)}) custom-call(bf16[256,128]{1,0:T(8,128)(2,1)S(1)} %get-tuple-element.42.refs_0_, bf16[256,128]{1,0:T(8,128)(2,1)S(1)} %get-tuple-element.43.refs_1_, f32[3,64,128]{2,1,0:T(8,128)S(1)} %get-tuple-element.44.refs_2_, bf16[128,256]{1,0:T(8,128)(2,1)S(1)} %get-tuple-element.45.refs_3_, ...), custom_call_target="tpu_custom_call" | custom-call | tf_op jit(solution)/shard_map/modes/pallas_call | solution.py:304
  35.3 9.7 %all-to-all-done.1 = bf16[448,2,128]{2,1,0:T(2,128)(2,1)S(1)} async-done(((bf16[448,2,128]{2,1,0:T(2,128)(2,1)}), bf16[448,2,128]{2,1,0:T(2,128)(2,1)S(1)}, u32[]{:S(2)}, u32[]{:S(2)}) %all-to-all-start.1) | async-done | bytes 229408 | tf_op jit(solution)/shard_map/all_to_all | solution.py:302
  45.0 0.0 copy-done
  45.0 0.8 %unpack.1 = (bf16[128,256]{1,0:T(8,128)(2,1)}, bf16[128,256]{1,0:T(8,128)(2,1)}, bf16[128,256]{1,0:T(8,128)(2,1)}, f32[16,128]{1,0:T(8,128)}) custom-call(bf16[896,128]{1,0:T(8,128)(2,1)S(1)} %bitcast.10, bf16[128,256]{1,0:T(8,128)(2,1)S(1)} %copy-done), custom_call_target="tpu_custom_call" | custom-call | tf_op jit(solution)/shard_map/unpack/pallas_call | solution.py:310
  (2 shorter events, 0.0 us)
Async XLA Ops:
  2.4 23.9 %all-to-all-start = ((bf16[192,4,128]{2,1,0:T(4,128)(2,1)}), bf16[192,4,128]{2,1,0:T(4,128)(2,1)S(1)}, u32[]{:S(2)}, u32[]{:S(2)}) async-start(bf16[192,4,128]{2,1,0:T(4,128)(2,1)} %bitcast.15), calls=%async_computation | async-start | bytes 393216 | tf_op jit(solution)/shard_map/all_to_all | solution.py:278
  15.4 0.7 %copy-start.1 = (bf16[128,16]{0,1:T(8,128)(2,1)S(1)}, bf16[128,16]{0,1:T(8,128)(2,1)}, u32[]{:S(2)}) copy-start(bf16[128,16]{0,1:T(8,128)(2,1)} %param.11) | copy-start | bytes 12292
  15.4 0.7 %copy-start.2 = (f32[16,4]{0,1:T(4,128)S(1)}, f32[16,4]{0,1:T(4,128)}, u32[]{:S(2)}) copy-start(f32[16,4]{0,1:T(4,128)} %param.13) | copy-start | bytes 772
  15.4 0.7 %copy-start.3 = (f32[16,4]{0,1:T(4,128)S(1)}, f32[16,4]{0,1:T(4,128)}, u32[]{:S(2)}) copy-start(f32[16,4]{0,1:T(4,128)} %param.12) | copy-start | bytes 772
  28.1 16.8 %all-to-all-start.1 = ((bf16[448,2,128]{2,1,0:T(2,128)(2,1)}), bf16[448,2,128]{2,1,0:T(2,128)(2,1)S(1)}, u32[]{:S(2)}, u32[]{:S(2)}) async-start(bf16[448,2,128]{2,1,0:T(2,128)(2,1)} %bitcast.5), calls=%async_computation.1 | async-start | bytes 458752 | tf_op jit(solution)/shard_map/all_to_all | solution.py:302
  33.8 11.1 %copy-start = (bf16[128,256]{1,0:T(8,128)(2,1)S(1)}, bf16[128,256]{1,0:T(8,128)(2,1)}, u32[]{:S(2)}) copy-start(bf16[128,256]{1,0:T(8,128)(2,1)} %refs_1_.1) | copy-start | bytes 196612

commit v2 on v1

--- a/solution.py
+++ b/solution.py
@@ -63,19 +63,29 @@
     return total
 
 
-def pack_kernel(x_ref, k_ref, q_ref, dy_ref, out_ref):
-    gated = rounded(q_ref[...].astype(F32) * dy_ref[...].astype(F32))
-    tiles = (x_ref.shape[1] // 8, 8, x_ref.shape[0])
-    x = x_ref[...].astype(F32).T.reshape(tiles)
-    k = pltpu.roll(k_ref[...].astype(F32).T.reshape(tiles), 4, 1)
+def pack_into(x, k, q, dy, out_ref):
+    tiles = (x.shape[1] // 8, 8, x.shape[0])
+    gated = rounded(q.astype(F32) * dy.astype(F32))
+    x = x.astype(F32).T.reshape(tiles)
+    k = pltpu.roll(k.astype(F32).T.reshape(tiles), 4, 1)
     d = gated.T.reshape(tiles)
     low = iota(tiles, 1) < 4
     rows = jnp.stack([jnp.where(low, x, k), jnp.where(low, d, x), jnp.where(low, k, d)], axis=1)
     out_ref[...] = rows.reshape(out_ref.shape).astype(BF16)
 
 
-def tables_kernel(rates_ref, residues_ref, filt_ref, pick_ref, fwd_ref, bwd_ref, hf_ref, hb_ref,
-                  aa_ref, bb_ref, am_ref, bm_ref, g_ref, w_ref, e_ref, lanes_ref):
+def front_kernel(*refs):
+    sources, results, held, done = refs[:7], refs[7:20], refs[20:27], refs[27]
+    copies = [pltpu.make_async_copy(sources[i], held[i], done.at[i]) for i in range(len(sources))]
+    for copy in copies:
+        copy.start()
+    for copy in copies:
+        copy.wait()
+    x_ref, k_ref, q_ref, dy_ref, rates_ref, residues_ref, filt_ref = held
+    (out_ref, fwd_ref, bwd_ref, hf_ref, hb_ref, aa_ref, bb_ref, am_ref, bm_ref, g_ref, w_ref,
+     e_ref, lanes_ref) = results
+    pack_into(x_ref[...], k_ref[...], q_ref[...], dy_ref[...], out_ref)
+
     def spread(ref):
         columns = ref[...].T
         return jnp.concatenate(
@@ -121,7 +131,10 @@
         high, low = halves(jnp.where(upper, band, 0.0))
         hf_ref[c] = jnp.concatenate([high, low], axis=0)
         hb_ref[c] = jnp.concatenate([high, low], axis=1)
-    taps = dot(pick_ref[...], filt_ref[...])[0:1]
+    share = lax.axis_size("ctx") // filt_ref.shape[0]
+    group = lax.axis_index("ctx") // share
+    pick = (iota((8, filt_ref.shape[0]), 1) == group).astype(BF16)
+    taps = dot(pick, filt_ref[...])[0:1]
     band = pltpu.roll(jnp.broadcast_to(taps, square), 0, 1, stride=1, stride_axis=0)
     same = jnp.where(upper, band, 0.0).astype(BF16)
     last = jnp.where(upper, 0.0, band).astype(BF16)
@@ -129,8 +142,8 @@
     bwd_ref[...] = jnp.concatenate([same, last], axis=1)
 
 
-def main_kernel(in_ref, fwd_ref, bwd_ref, hf_ref, hb_ref, aa_ref, bb_ref, g_ref, w_ref, lanes_ref,
-                out_ref, u_ref, d_ref, s_ref, in32, out32):
+def main_kernel(in_ref, fwd_ref, bwd_ref, hf_ref, hb_ref, aa_ref, bb_ref, am_ref, bm_ref, g_ref, w_ref,
+                e_ref, lanes_ref, out_ref, sums_ref, in32, out32):
     count = in_ref.shape[0] // IN_ROWS
     rows = OWN * count
     in32[...] = in_ref[...].astype(F32)
@@ -151,8 +164,6 @@
     v = rounded(dot(xx, fwd_ref[...]))
     u = (k * v).astype(BF16)
     d = d.astype(BF16)
-    u_ref[...] = u
-    d_ref[...] = d
     uu = jnp.concatenate([u, u], axis=1)
     dd = jnp.concatenate([d, d], axis=1)
     moment_u = pick_own(dot(uu, aa_ref[...], NT), count)
@@ -167,9 +178,6 @@
         ahead = ahead + factor * jnp.where(at < by, 0.0, pltpu.roll(ahead, by, 0))
         behind = behind + factor * jnp.where(at >= count - by, 0.0, pltpu.roll(behind, count - by, 0))
         by *= 2
-    s_ref[0] = ahead
-    s_ref[1] = behind
-    s_ref[2] = moment_d
 
     def states(value):
         high = rounded(value)
@@ -200,12 +208,13 @@
     out32[pl.ds(3 * OWN, count, stride=OUT_ROWS), :] = jnp.broadcast_to(high, (count, CHUNK))
     out32[pl.ds(3 * OWN + 1, count, stride=OUT_ROWS), :] = jnp.broadcast_to(sums - high, (count, CHUNK))
     out_ref[...] = out32[...].astype(BF16)
-
-
-def modes_kernel(scale, u_ref, d_ref, s_ref, am_ref, bm_ref, e_ref, lanes_ref, residue_ref, rate_ref):
-    count = s_ref.shape[1]
+    first, second = mode_sums(u, d, ahead, behind, moment_d, am_ref, bm_ref, e_ref, lanes_ref)
+    sums_ref[...] = jnp.concatenate([first, second, jnp.zeros((6, LANES), F32)], axis=0)
+
+
+def mode_sums(u, d, ahead, behind, moment_d, am_ref, bm_ref, e_ref, lanes_ref):
+    count = ahead.shape[0]
     keep = causal((CHUNK, CHUNK))
-    u, d = u_ref[...], d_ref[...]
     u_mirrored = mirrored(u)
     cots = []
     for c in range(OWN):
@@ -218,8 +227,7 @@
     inner = jnp.sum(inner, axis=0, keepdims=True)
     slope_u = pick_own(dot(jnp.concatenate([u, u], axis=1), am_ref[...], NT), count)
     slope_d = pick_own(dot(jnp.concatenate([d, d], axis=1), bm_ref[...], NT), count)
-    rates, residues = lanes_ref[0:1, :], lanes_ref[1:2, :]
-    ahead, behind, moment_d = s_ref[0], s_ref[1], s_ref[2]
+    rates = lanes_ref[0:1, :]
     first = jnp.sum(ahead * moment_d, axis=0, keepdims=True)
     second = jnp.sum(
         ahead * slope_d + slope_u * behind + (CHUNK * jnp.exp(-CHUNK * rates)) * (ahead * behind),
@@ -228,6 +236,12 @@
     half = iota((1, LANES), 1) < LANES // 2
     first = first + jnp.where(half, inner, pltpu.roll(inner, LANES // 2, 1))
     second = second + jnp.where(half, pltpu.roll(inner, LANES // 2, 1), inner)
+    return first, second
+
+
+def mode_results(scale, sums_ref, lanes_ref, residue_ref, rate_ref):
+    first, second = sums_ref[0:1, :], sums_ref[1:2, :]
+    rates, residues = lanes_ref[0:1, :], lanes_ref[1:2, :]
     norm = jnp.sqrt(2.0 * rates / MODES)
     results = ((residue_ref, norm * first * scale),
                (rate_ref, residues * norm * (0.5 * first - rates * second) * scale))
@@ -236,7 +250,9 @@
             ref[c : c + 1, :] = value[:, c * MODES : (c + 1) * MODES]
 
 
-def unpack_kernel(scale, in_ref, dy_ref, dx_ref, dq_ref, dk_ref, filt_ref, in32, mid32, sum32):
+def unpack_kernel(scale, in_ref, dy_ref, sums_ref, lanes_ref, dx_ref, dq_ref, dk_ref, filt_ref,
+                  residue_ref, rate_ref, in32, mid32, sum32):
+    mode_results(scale, sums_ref, lanes_ref, residue_ref, rate_ref)
     count = in_ref.shape[0] // OUT_ROWS
     in32[...] = in_ref[...].astype(F32)
 
@@ -267,53 +283,45 @@
 def local(x, out_gate, in_gate, out_cot, mr_filter, residues, rates):
     tokens, chans = x.shape
     peers = lax.axis_size("ctx")
-    groups = mr_filter.shape[1]
     scale = 1.0 / math.sqrt(tokens * peers)
-    rows = OWN * peers
     square2 = (CHUNK, 2 * CHUNK)
     tall2 = (2 * CHUNK, CHUNK)
 
-    packed = pl.pallas_call(pack_kernel, out_shape=shape((peers * IN_ROWS, CHUNK), BF16), name="pack")(
-        x, in_gate, out_gate, out_cot)
-    arrived = lax.all_to_all(packed.reshape(3 * peers, OWN, CHUNK), "ctx", split_axis=0, concat_axis=0, tiled=True)
-
-    group = lax.axis_index("ctx") * groups // peers
-    pick = (lax.broadcasted_iota(jnp.int32, (8, groups), 1) == group).astype(BF16)
-    fwd, bwd, hf, hb, aa, bb, am, bm, g, w, e, lanes = pl.pallas_call(
-        tables_kernel,
+    sources = (x, in_gate, out_gate, out_cot, rates.T, residues.T, mr_filter.T)
+    packed, fwd, bwd, hf, hb, aa, bb, am, bm, g, w, e, lanes = pl.pallas_call(
+        front_kernel,
         out_shape=(
-            shape(tall2, BF16), shape(square2, BF16),
+            shape((peers * IN_ROWS, CHUNK), BF16), shape(tall2, BF16), shape(square2, BF16),
             shape((OWN,) + tall2, BF16), shape((OWN,) + square2, BF16),
             shape(square2, BF16), shape(square2, BF16), shape(square2, BF16), shape(square2, BF16),
             shape(tall2, BF16), shape(tall2, BF16),
             shape((LANES, CHUNK), F32), shape((8, LANES), F32),
         ),
-        compiler_params=ROOM, name="tables",
-    )(rates.T, residues.T, mr_filter.T, pick)
-
-    back, u, d, states = pl.pallas_call(
+        in_specs=[pl.BlockSpec(memory_space=pltpu.HBM)] * len(sources),
+        scratch_shapes=[pltpu.VMEM(source.shape, source.dtype) for source in sources]
+        + [pltpu.SemaphoreType.DMA((len(sources),))],
+        compiler_params=ROOM, name="front",
+    )(*[pltpu.with_memory_space_constraint(source, pltpu.HBM) for source in sources])
+    arrived = lax.all_to_all(packed.reshape(3 * peers, OWN, CHUNK), "ctx", split_axis=0, concat_axis=0, tiled=True)
+
+    back, sums = pl.pallas_call(
         main_kernel,
-        out_shape=(shape((peers * OUT_ROWS, CHUNK), BF16), shape((rows, CHUNK), BF16),
-                   shape((rows, CHUNK), BF16), shape((3, peers, LANES), F32)),
+        out_shape=(shape((peers * OUT_ROWS, CHUNK), BF16), shape((8, LANES), F32)),
         scratch_shapes=[pltpu.VMEM((peers * IN_ROWS, CHUNK), F32), pltpu.VMEM((peers * OUT_ROWS, CHUNK), F32)],
         compiler_params=ROOM, name="mixer",
-    )(arrived.reshape(peers * IN_ROWS, CHUNK), fwd, bwd, hf, hb, aa, bb, g, w, lanes)
+    )(arrived.reshape(peers * IN_ROWS, CHUNK), fwd, bwd, hf, hb, aa, bb, am, bm, g, w, e, lanes)
 
     returned = lax.all_to_all(back.reshape(peers * OUT_ROWS // 2, 2, CHUNK), "ctx", split_axis=0, concat_axis=0, tiled=True)
 
-    residue_grad, rate_grad = pl.pallas_call(
-        lambda *refs: modes_kernel(scale, *refs),
-        out_shape=(shape(residues.shape[::-1], F32), shape(rates.shape[::-1], F32)),
-        compiler_params=ROOM, name="modes",
-    )(u, d, states, am, bm, e, lanes)
-
-    input_grad, out_gate_grad, in_gate_grad, filter_grad = pl.pallas_call(
+    input_grad, out_gate_grad, in_gate_grad, filter_grad, residue_grad, rate_grad = pl.pallas_call(
         lambda *refs: unpack_kernel(scale, *refs),
-        out_shape=(shape(x.shape, BF16), shape(x.shape, BF16), shape(x.shape, BF16), shape(mr_filter.shape[::-1], F32)),
+        out_shape=(shape(x.shape, BF16), shape(x.shape, BF16), shape(x.shape, BF16),
+                   shape(mr_filter.shape[::-1], F32),
+                   shape(residues.shape[::-1], F32), shape(rates.shape[::-1], F32)),
         scratch_shapes=[pltpu.VMEM((peers * OUT_ROWS, CHUNK), F32), pltpu.VMEM((3, chans, CHUNK), F32),
                         pltpu.VMEM((peers, CHUNK), F32)],
         compiler_params=ROOM, name="unpack",
-    )(returned.reshape(peers * OUT_ROWS, CHUNK), out_cot)
+    )(returned.reshape(peers * OUT_ROWS, CHUNK), out_cot, sums, lanes)
     return (input_grad, out_gate_grad, in_gate_grad, filter_grad.T, residue_grad.T, rate_grad.T)
 
 

time: 46.1 us -> 45.1 us (0.978)
  blocking collectives: 0 us -> 40.5 us
  waiting for transfers between devices: 19.5 us -> 0 us
  starting transfers between devices: 18.7 us -> 0 us
  Pallas kernels: 6.14 us -> 3.76 us
  local copies, waits for them, and re-layouts: 0.69 us -> 0.01 us
    all_to_all x0 -> x2, blocking collectives: none -> 40.5 us  [the longest x1 23.7 us: local(): lax.all_to_all(packed.reshape(3 * peers, OWN, CHUNK), 'ctx', split_axis=0...]
    all_to_all x2 -> x0, waiting for transfers between devices: 19.5 us -> none  [the longest x1 9.87 us: local(): lax.all_to_all(packed.reshape(3 * peers, OWN, CHUNK), 'ctx', split_axis=0...]
    all_to_all x2 -> x0, starting transfers between devices: 18.7 us -> none  [the longest x1 13 us: local(): lax.all_to_all(packed.reshape(3 * peers, OWN, CHUNK), 'ctx', split_axis=0...]
    pallas_call x3 -> x1, Pallas kernels: 3.51 us -> 1.39 us  [local(): pl.pallas_call(front_kernel, out_shape=(shape((peers * IN_ROWS, CHUNK), B...]
    unnamed x8 -> x2, local copies, waits for them, and re-layouts: 0.69 us -> 0.01 us
  transfers between devices with their start and end apart: 2 -> 0, of which waited for: 2 -> 0; matrix products, arithmetic and copies ran while one was open for 0% -> 0% of each run, Pallas kernels for 4% -> 0%
where the time goes in v2:
time: 45.1 us; the launch traced here: 44.9 us
  blocking collectives  40.5 us (90%)
  Pallas kernels  3.76 us (8%)
  between operations  0.64 us (1%)
    all_to_all x1, blocking collectives, local(): lax.all_to_all(packed.reshape(3 * peers, OWN, CHUNK), 'ctx', split_axis=0...  23.7 us
    all_to_all x1, blocking collectives, local(): lax.all_to_all(back.reshape(peers * OUT_ROWS // 2, 2, CHUNK), 'ctx', spli...  16.8 us
    pallas_call x1, Pallas kernels, local(): pl.pallas_call(main_kernel, out_shape=(shape((peers * OUT_ROWS, CHUNK), B...  1.53 us
    pallas_call x1, Pallas kernels, local(): pl.pallas_call(front_kernel, out_shape=(shape((peers * IN_ROWS, CHUNK), B...  1.39 us

profile of v2, /device:TPU:1, one launch (start us, length us, event | category | flops | bytes accessed | tf_op | source)
XLA Modules:
  0.0 44.9 jit_solution(2459057646763604191)
XLA Ops:
  0.6 1.4 %front.1 = (bf16[768,128]{1,0:T(8,128)(2,1)S(1)}, bf16[256,128]{1,0:T(8,128)(2,1)S(1)}, bf16[128,256]{1,0:T(8,128)(2,1)S(1)}, bf16[4,256,128]{2,1,0:T(8,128)(2,1...) custom-call(bf16[128,256]{1,0:T(8,128)(2,1)} %refs_0_.1, ...), custom_call_target="tpu_custom_call" | custom-call | tf_op jit(solution)/shard_map/front/pallas_call | solution.py:291
  2.0 23.7 %all_to_all.10 = bf16[192,4,128]{2,1,0:T(4,128)(2,1)S(1)} all-to-all(bf16[192,4,128]{2,1,0:T(4,128)(2,1)S(1)} %bitcast.13), channel_id=1, replica_groups=mesh['ctx'=64,'ch'=4] {'ctx'}, dimensions={0} | all-to-all | bytes 393216 | tf_op jit(solution)/shard_map/all_to_all | solution.py:305
  25.8 1.5 %mixer.1 = (bf16[896,128]{1,0:T(8,128)(2,1)S(1)}, f32[8,128]{1,0:T(8,128)S(1)}) custom-call(bf16[768,128]{1,0:T(8,128)(2,1)S(1)} %bitcast.11, bf16[256,128]{1,0:T(8,128)(2,1)S(1)} %get-tuple-element.28.fwd_ref, bf16[128,256]{1,0:T(8,128)(2,1)S(1)} %get-tuple-element.29.bwd_ref, bf16[4,256,128]{2,1,0:T(8,128)(2,1)S(1)} %get-tuple-element.30.hf_ref, ...), custom_call_target="tpu_custom_call" | custom-call | tf_op jit(solution)/shard_map/mixer/pallas_call | solution.py:307
  27.3 0.0 copy-start
  27.3 16.8 %all_to_all.11 = bf16[448,2,128]{2,1,0:T(2,128)(2,1)S(1)} all-to-all(bf16[448,2,128]{2,1,0:T(2,128)(2,1)S(1)} %bitcast.12), channel_id=1, replica_groups=mesh['ctx'=64,'ch'=4] {'ctx'}, dimensions={0} | all-to-all | bytes 458752 | tf_op jit(solution)/shard_map/all_to_all | solution.py:314
  44.1 0.0 copy-done
  44.1 0.8 %unpack.1 = (bf16[128,256]{1,0:T(8,128)(2,1)}, bf16[128,256]{1,0:T(8,128)(2,1)}, bf16[128,256]{1,0:T(8,128)(2,1)}, f32[16,128]{1,0:T(8,128)}, f32[4,16]{1,0:T(4,128)}, /*index=5*/f32[4,16]{1,0:T(4,128)}) custom-call(bf16[896,128]{1,0:T(8,128)(2,1)S(1)} %bitcast.10, bf16[128,256]{1,0:T(8,128)(2,1)S(1)} %copy-done, f32[8,128]{1,0:T(8,128)S(1)} %get-tuple-element.41.refs_2_, ...), custom_call_target="tpu_custom_call" | custom-call | tf_op jit(solution)/shard_map/unpack/pallas_call | solution.py:316
Async XLA Ops:
  27.3 16.8 %copy-start = (bf16[128,256]{1,0:T(8,128)(2,1)S(1)}, bf16[128,256]{1,0:T(8,128)(2,1)}, u32[]{:S(2)}) copy-start(bf16[128,256]{1,0:T(8,128)(2,1)} %refs_1_.3) | copy-start | bytes 196612

commit v3 on v2

--- a/solution.py
+++ b/solution.py
@@ -75,16 +75,16 @@
 
 
 def front_kernel(*refs):
-    sources, results, held, done = refs[:7], refs[7:20], refs[20:27], refs[27]
+    sources, results, held, done = refs[:7], refs[7:18], refs[18:25], refs[25]
     copies = [pltpu.make_async_copy(sources[i], held[i], done.at[i]) for i in range(len(sources))]
-    for copy in copies:
+    large, small = copies[:4], copies[4:]
+    for copy in small + large:
         copy.start()
-    for copy in copies:
+    for copy in small:
         copy.wait()
     x_ref, k_ref, q_ref, dy_ref, rates_ref, residues_ref, filt_ref = held
-    (out_ref, fwd_ref, bwd_ref, hf_ref, hb_ref, aa_ref, bb_ref, am_ref, bm_ref, g_ref, w_ref,
+    (out_ref, fwd_ref, bwd_ref, hf_ref, hb_ref, aa_ref, bb_ref, g_ref, w_ref,
      e_ref, lanes_ref) = results
-    pack_into(x_ref[...], k_ref[...], q_ref[...], dy_ref[...], out_ref)
 
     def spread(ref):
         columns = ref[...].T
@@ -106,17 +106,15 @@
     decay = jnp.exp(-rates * step)
     after = jnp.exp(-rates * (step + 1.0))
     before = jnp.exp(-rates * (CHUNK - 1.0 - step))
-    e_ref[0 : OWN * MODES, :] = decay
-    e_ref[OWN * MODES :, :] = decay * step
+    high, low = halves(jnp.concatenate([decay, decay * step], axis=0))
+    e_ref[...] = jnp.concatenate([high, low], axis=1)
 
     def wide(value):
         high, low = halves(value)
         return jnp.concatenate([jnp.concatenate([high, low], axis=1)] * 2, axis=0)
 
-    aa_ref[...] = wide(before)
-    bb_ref[...] = wide(after)
-    am_ref[...] = wide(before * (CHUNK - 1.0 - step))
-    bm_ref[...] = wide(after * (step + 1.0))
+    aa_ref[...] = jnp.concatenate([wide(before), wide(before * (CHUNK - 1.0 - step))], axis=0)
+    bb_ref[...] = jnp.concatenate([wide(after), wide(after * (step + 1.0))], axis=0)
 
     def tall(value):
         high, low = halves(value)
@@ -140,9 +138,12 @@
     last = jnp.where(upper, 0.0, band).astype(BF16)
     fwd_ref[...] = jnp.concatenate([same, last], axis=0)
     bwd_ref[...] = jnp.concatenate([same, last], axis=1)
-
-
-def main_kernel(in_ref, fwd_ref, bwd_ref, hf_ref, hb_ref, aa_ref, bb_ref, am_ref, bm_ref, g_ref, w_ref,
+    for copy in large:
+        copy.wait()
+    pack_into(x_ref[...], k_ref[...], q_ref[...], dy_ref[...], out_ref)
+
+
+def main_kernel(in_ref, fwd_ref, bwd_ref, hf_ref, hb_ref, aa_ref, bb_ref, g_ref, w_ref,
                 e_ref, lanes_ref, out_ref, sums_ref, in32, out32):
     count = in_ref.shape[0] // IN_ROWS
     rows = OWN * count
@@ -166,8 +167,11 @@
     d = d.astype(BF16)
     uu = jnp.concatenate([u, u], axis=1)
     dd = jnp.concatenate([d, d], axis=1)
-    moment_u = pick_own(dot(uu, aa_ref[...], NT), count)
-    moment_d = pick_own(dot(dd, bb_ref[...], NT), count)
+    moment_u = dot(uu, aa_ref[...], NT)
+    moment_d = dot(dd, bb_ref[...], NT)
+    slope_u, slope_d = moment_u[:, LANES:], moment_d[:, LANES:]
+    moment_u = pick_own(moment_u[:, :LANES], count)
+    moment_d = pick_own(moment_d[:, :LANES], count)
     at = iota((count, LANES), 0)
     rates = lanes_ref[0:1, :]
     ahead = jnp.where(at < 1, 0.0, pltpu.roll(moment_u, 1, 0))
@@ -201,18 +205,17 @@
     dv = dv.astype(BF16)
     dvv = jnp.concatenate([dv, dv_next.astype(BF16)], axis=1)
     put(2, dot(dvv, bwd_ref[...], NT))
-    same = dot(dv, mirrored(xx[:, :CHUNK]), TN)
-    last = dot(dv, mirrored(xx[:, CHUNK:]), TN)
-    sums = diagonal_sums(jnp.where(causal((CHUNK, CHUNK)), same, last))
+    cross = dot(dv, jnp.concatenate([mirrored(xx[:, :CHUNK]), mirrored(xx[:, CHUNK:])], axis=1), TN)
+    sums = diagonal_sums(jnp.where(causal((CHUNK, CHUNK)), cross[:, :CHUNK], cross[:, CHUNK:]))
     high = rounded(sums)
     out32[pl.ds(3 * OWN, count, stride=OUT_ROWS), :] = jnp.broadcast_to(high, (count, CHUNK))
     out32[pl.ds(3 * OWN + 1, count, stride=OUT_ROWS), :] = jnp.broadcast_to(sums - high, (count, CHUNK))
     out_ref[...] = out32[...].astype(BF16)
-    first, second = mode_sums(u, d, ahead, behind, moment_d, am_ref, bm_ref, e_ref, lanes_ref)
+    first, second = mode_sums(u, d, ahead, behind, moment_d, slope_u, slope_d, e_ref, lanes_ref)
     sums_ref[...] = jnp.concatenate([first, second, jnp.zeros((6, LANES), F32)], axis=0)
 
 
-def mode_sums(u, d, ahead, behind, moment_d, am_ref, bm_ref, e_ref, lanes_ref):
+def mode_sums(u, d, ahead, behind, moment_d, slope_u, slope_d, e_ref, lanes_ref):
     count = ahead.shape[0]
     keep = causal((CHUNK, CHUNK))
     u_mirrored = mirrored(u)
@@ -220,13 +223,13 @@
     for c in range(OWN):
         part = slice(c * count, (c + 1) * count)
         cots.append(diagonal_sums(jnp.where(keep, dot(d[part], u_mirrored[part], TN), 0.0)))
-    cots = jnp.concatenate(cots + [jnp.zeros((8 - OWN, CHUNK), F32)], axis=0)
-    inner = lax.dot_general(cots, e_ref[...], NT, precision=lax.Precision.HIGHEST,
-                            preferred_element_type=F32)
-    inner = jnp.where((iota(inner.shape, 1) % (OWN * MODES)) // MODES == iota(inner.shape, 0), inner, 0.0)
+    cots = jnp.concatenate(cots, axis=0)
+    high = rounded(cots)
+    cots = jnp.concatenate([high, cots - high], axis=0).astype(BF16)
+    inner = dot(jnp.concatenate([cots, cots], axis=1), e_ref[...], NT)
+    inner = jnp.where((iota(inner.shape, 1) % (OWN * MODES)) // MODES == iota(inner.shape, 0) % OWN, inner, 0.0)
     inner = jnp.sum(inner, axis=0, keepdims=True)
-    slope_u = pick_own(dot(jnp.concatenate([u, u], axis=1), am_ref[...], NT), count)
-    slope_d = pick_own(dot(jnp.concatenate([d, d], axis=1), bm_ref[...], NT), count)
+    slope_u, slope_d = pick_own(slope_u, count), pick_own(slope_d, count)
     rates = lanes_ref[0:1, :]
     first = jnp.sum(ahead * moment_d, axis=0, keepdims=True)
     second = jnp.sum(
@@ -288,14 +291,14 @@
     tall2 = (2 * CHUNK, CHUNK)
 
     sources = (x, in_gate, out_gate, out_cot, rates.T, residues.T, mr_filter.T)
-    packed, fwd, bwd, hf, hb, aa, bb, am, bm, g, w, e, lanes = pl.pallas_call(
+    packed, fwd, bwd, hf, hb, aa, bb, g, w, e, lanes = pl.pallas_call(
         front_kernel,
         out_shape=(
             shape((peers * IN_ROWS, CHUNK), BF16), shape(tall2, BF16), shape(square2, BF16),
             shape((OWN,) + tall2, BF16), shape((OWN,) + square2, BF16),
-            shape(square2, BF16), shape(square2, BF16), shape(square2, BF16), shape(square2, BF16),
+            shape((2 * CHUNK, 2 * CHUNK), BF16), shape((2 * CHUNK, 2 * CHUNK), BF16),
             shape(tall2, BF16), shape(tall2, BF16),
-            shape((LANES, CHUNK), F32), shape((8, LANES), F32),
+            shape(square2, BF16), shape((8, LANES), F32),
         ),
         in_specs=[pl.BlockSpec(memory_space=pltpu.HBM)] * len(sources),
         scratch_shapes=[pltpu.VMEM(source.shape, source.dtype) for source in sources]
@@ -309,7 +312,7 @@
         out_shape=(shape((peers * OUT_ROWS, CHUNK), BF16), shape((8, LANES), F32)),
         scratch_shapes=[pltpu.VMEM((peers * IN_ROWS, CHUNK), F32), pltpu.VMEM((peers * OUT_ROWS, CHUNK), F32)],
         compiler_params=ROOM, name="mixer",
-    )(arrived.reshape(peers * IN_ROWS, CHUNK), fwd, bwd, hf, hb, aa, bb, am, bm, g, w, e, lanes)
+    )(arrived.reshape(peers * IN_ROWS, CHUNK), fwd, bwd, hf, hb, aa, bb, g, w, e, lanes)
 
     returned = lax.all_to_all(back.reshape(peers * OUT_ROWS // 2, 2, CHUNK), "ctx", split_axis=0, concat_axis=0, tiled=True)
 

time: 45.1 us -> 44.6 us (0.989)
  Pallas kernels: 3.76 us -> 3.3 us
where the time goes in v3:
time: 44.6 us; the launch traced here: 44.4 us
  blocking collectives  40.5 us (91%)
  Pallas kernels  3.3 us (7%)
  between operations  0.64 us (1%)
    all_to_all x1, blocking collectives, local(): lax.all_to_all(packed.reshape(3 * peers, OWN, CHUNK), 'ctx', split_axis=0...  23.7 us
    all_to_all x1, blocking collectives, local(): lax.all_to_all(back.reshape(peers * OUT_ROWS // 2, 2, CHUNK), 'ctx', spli...  16.8 us
    pallas_call x1, Pallas kernels, local(): pl.pallas_call(front_kernel, out_shape=(shape((peers * IN_ROWS, CHUNK), B...  1.26 us
    pallas_call x1, Pallas kernels, local(): pl.pallas_call(main_kernel, out_shape=(shape((peers * OUT_ROWS, CHUNK), B...  1.19 us

profile of v3, /device:TPU:1, one launch (start us, length us, event | category | flops | bytes accessed | tf_op | source)
XLA Modules:
  0.0 44.4 jit_solution(2047888967433115009)
XLA Ops:
  0.6 1.3 %front.1 = (bf16[768,128]{1,0:T(8,128)(2,1)S(1)}, bf16[256,128]{1,0:T(8,128)(2,1)S(1)}, bf16[128,256]{1,0:T(8,128)(2,1)S(1)}, bf16[4,256,128]{2,1,0:T(8,128)(2,1...) custom-call(bf16[128,256]{1,0:T(8,128)(2,1)} %refs_0_.1, ...), custom_call_target="tpu_custom_call" | custom-call | tf_op jit(solution)/shard_map/front/pallas_call | solution.py:294
  1.9 23.7 %all_to_all.10 = bf16[192,4,128]{2,1,0:T(4,128)(2,1)S(1)} all-to-all(bf16[192,4,128]{2,1,0:T(4,128)(2,1)S(1)} %bitcast.13), channel_id=1, replica_groups=mesh['ctx'=64,'ch'=4] {'ctx'}, dimensions={0} | all-to-all | bytes 393216 | tf_op jit(solution)/shard_map/all_to_all | solution.py:308
  25.6 1.2 %mixer.1 = (bf16[896,128]{1,0:T(8,128)(2,1)S(1)}, f32[8,128]{1,0:T(8,128)S(1)}) custom-call(bf16[768,128]{1,0:T(8,128)(2,1)S(1)} %bitcast.11, bf16[256,128]{1,0:T(8,128)(2,1)S(1)} %get-tuple-element.26.fwd_ref, bf16[128,256]{1,0:T(8,128)(2,1)S(1)} %get-tuple-element.27.bwd_ref, bf16[4,256,128]{2,1,0:T(8,128)(2,1)S(1)} %get-tuple-element.28.hf_ref, ...), custom_call_target="tpu_custom_call" | custom-call | tf_op jit(solution)/shard_map/mixer/pallas_call | solution.py:310
  26.8 0.0 copy-start
  26.8 16.8 %all_to_all.11 = bf16[448,2,128]{2,1,0:T(2,128)(2,1)S(1)} all-to-all(bf16[448,2,128]{2,1,0:T(2,128)(2,1)S(1)} %bitcast.12), channel_id=1, replica_groups=mesh['ctx'=64,'ch'=4] {'ctx'}, dimensions={0} | all-to-all | bytes 458752 | tf_op jit(solution)/shard_map/all_to_all | solution.py:317
  43.6 0.0 copy-done
  43.6 0.8 %unpack.1 = (bf16[128,256]{1,0:T(8,128)(2,1)}, bf16[128,256]{1,0:T(8,128)(2,1)}, bf16[128,256]{1,0:T(8,128)(2,1)}, f32[16,128]{1,0:T(8,128)}, f32[4,16]{1,0:T(4,128)}, /*index=5*/f32[4,16]{1,0:T(4,128)}) custom-call(bf16[896,128]{1,0:T(8,128)(2,1)S(1)} %bitcast.10, bf16[128,256]{1,0:T(8,128)(2,1)S(1)} %copy-done, f32[8,128]{1,0:T(8,128)S(1)} %get-tuple-element.37.refs_2_, ...), custom_call_target="tpu_custom_call" | custom-call | tf_op jit(solution)/shard_map/unpack/pallas_call | solution.py:319
Async XLA Ops:
  26.8 16.8 %copy-start = (bf16[128,256]{1,0:T(8,128)(2,1)S(1)}, bf16[128,256]{1,0:T(8,128)(2,1)}, u32[]{:S(2)}) copy-start(bf16[128,256]{1,0:T(8,128)(2,1)} %refs_1_.3) | copy-start | bytes 196612

commit v4 on v3

--- a/solution.py
+++ b/solution.py
@@ -65,10 +65,10 @@
 
 def pack_into(x, k, q, dy, out_ref):
     tiles = (x.shape[1] // 8, 8, x.shape[0])
-    gated = rounded(q.astype(F32) * dy.astype(F32))
-    x = x.astype(F32).T.reshape(tiles)
-    k = pltpu.roll(k.astype(F32).T.reshape(tiles), 4, 1)
-    d = gated.T.reshape(tiles)
+    gated = (q.astype(F32) * dy.astype(F32)).astype(BF16)
+    x = x.T.astype(F32).reshape(tiles)
+    k = pltpu.roll(k.T.astype(F32).reshape(tiles), 4, 1)
+    d = gated.T.astype(F32).reshape(tiles)
     low = iota(tiles, 1) < 4
     rows = jnp.stack([jnp.where(low, x, k), jnp.where(low, d, x), jnp.where(low, k, d)], axis=1)
     out_ref[...] = rows.reshape(out_ref.shape).astype(BF16)
@@ -262,11 +262,11 @@
     def take(which):
         for c in range(OWN):
             mid32[which, pl.ds(c, count, stride=OWN), :] = in32[pl.ds(which * OWN + c, count, stride=OUT_ROWS), :]
-        return mid32[which].T
-
-    dq_ref[...] = (take(0) * dy_ref[...].astype(F32)).astype(BF16)
-    dk_ref[...] = take(1).astype(BF16)
-    dx_ref[...] = take(2).astype(BF16)
+        return mid32[which].astype(BF16).T
+
+    dq_ref[...] = (take(0).astype(F32) * dy_ref[...].astype(F32)).astype(BF16)
+    dk_ref[...] = take(1)
+    dx_ref[...] = take(2)
     sum32[...] = in32[pl.ds(3 * OWN, count, stride=OUT_ROWS), :] + in32[pl.ds(3 * OWN + 1, count, stride=OUT_ROWS), :]
     groups = filt_ref.shape[0]
     share = count // groups

time: 44.6 us -> 44.6 us (level)
  no operation moved by 1% of the time
where the time goes in v4:
time: 44.6 us; the launch traced here: 44.4 us
  blocking collectives  40.5 us (91%)
  Pallas kernels  3.25 us (7%)
  between operations  0.64 us (1%)
    all_to_all x1, blocking collectives, local(): lax.all_to_all(packed.reshape(3 * peers, OWN, CHUNK), 'ctx', split_axis=0...  23.7 us
    all_to_all x1, blocking collectives, local(): lax.all_to_all(back.reshape(peers * OUT_ROWS // 2, 2, CHUNK), 'ctx', spli...  16.8 us
    pallas_call x1, Pallas kernels, local(): pl.pallas_call(front_kernel, out_shape=(shape((peers * IN_ROWS, CHUNK), B...  1.24 us
    pallas_call x1, Pallas kernels, local(): pl.pallas_call(main_kernel, out_shape=(shape((peers * OUT_ROWS, CHUNK), B...  1.19 us

profile of v4, /device:TPU:1, one launch (start us, length us, event | category | flops | bytes accessed | tf_op | source)
XLA Modules:
  0.0 44.4 jit_solution(5018590539718260588)
XLA Ops:
  0.6 1.2 %front.1 = (bf16[768,128]{1,0:T(8,128)(2,1)S(1)}, bf16[256,128]{1,0:T(8,128)(2,1)S(1)}, bf16[128,256]{1,0:T(8,128)(2,1)S(1)}, bf16[4,256,128]{2,1,0:T(8,128)(2,1...) custom-call(bf16[128,256]{1,0:T(8,128)(2,1)} %refs_0_.1, ...), custom_call_target="tpu_custom_call" | custom-call | tf_op jit(solution)/shard_map/front/pallas_call | solution.py:294
  1.9 23.7 %all_to_all.10 = bf16[192,4,128]{2,1,0:T(4,128)(2,1)S(1)} all-to-all(bf16[192,4,128]{2,1,0:T(4,128)(2,1)S(1)} %bitcast.13), channel_id=1, replica_groups=mesh['ctx'=64,'ch'=4] {'ctx'}, dimensions={0} | all-to-all | bytes 393216 | tf_op jit(solution)/shard_map/all_to_all | solution.py:308
  25.6 1.2 %mixer.1 = (bf16[896,128]{1,0:T(8,128)(2,1)S(1)}, f32[8,128]{1,0:T(8,128)S(1)}) custom-call(bf16[768,128]{1,0:T(8,128)(2,1)S(1)} %bitcast.11, bf16[256,128]{1,0:T(8,128)(2,1)S(1)} %get-tuple-element.26.fwd_ref, bf16[128,256]{1,0:T(8,128)(2,1)S(1)} %get-tuple-element.27.bwd_ref, bf16[4,256,128]{2,1,0:T(8,128)(2,1)S(1)} %get-tuple-element.28.hf_ref, ...), custom_call_target="tpu_custom_call" | custom-call | tf_op jit(solution)/shard_map/mixer/pallas_call | solution.py:310
  26.8 0.0 copy-start
  26.8 16.8 %all_to_all.11 = bf16[448,2,128]{2,1,0:T(2,128)(2,1)S(1)} all-to-all(bf16[448,2,128]{2,1,0:T(2,128)(2,1)S(1)} %bitcast.12), channel_id=1, replica_groups=mesh['ctx'=64,'ch'=4] {'ctx'}, dimensions={0} | all-to-all | bytes 458752 | tf_op jit(solution)/shard_map/all_to_all | solution.py:317
  43.6 0.0 copy-done
  43.6 0.8 %unpack.1 = (bf16[128,256]{1,0:T(8,128)(2,1)}, bf16[128,256]{1,0:T(8,128)(2,1)}, bf16[128,256]{1,0:T(8,128)(2,1)}, f32[16,128]{1,0:T(8,128)}, f32[4,16]{1,0:T(4,128)}, /*index=5*/f32[4,16]{1,0:T(4,128)}) custom-call(bf16[896,128]{1,0:T(8,128)(2,1)S(1)} %bitcast.10, bf16[128,256]{1,0:T(8,128)(2,1)S(1)} %copy-done, f32[8,128]{1,0:T(8,128)S(1)} %get-tuple-element.37.refs_2_, ...), custom_call_target="tpu_custom_call" | custom-call | tf_op jit(solution)/shard_map/unpack/pallas_call | solution.py:319
Async XLA Ops:
  26.8 16.8 %copy-start = (bf16[128,256]{1,0:T(8,128)(2,1)S(1)}, bf16[128,256]{1,0:T(8,128)(2,1)}, u32[]{:S(2)}) copy-start(bf16[128,256]{1,0:T(8,128)(2,1)} %refs_1_.3) | copy-start | bytes 196612

commit v5 on v3

--- a/solution.py
+++ b/solution.py
@@ -55,6 +55,11 @@
     return (iota(shape, 1) % (OWN * MODES)) // MODES == channel
 
 
+def fold(value):
+    half = value.shape[1] // 2
+    return value[:, :half] + value[:, half:]
+
+
 def pick_own(table, count):
     total = jnp.zeros((count, LANES), F32)
     for channel in range(OWN):
@@ -75,7 +80,7 @@
 
 
 def front_kernel(*refs):
-    sources, results, held, done = refs[:7], refs[7:18], refs[18:25], refs[25]
+    sources, results, held, done = refs[:7], refs[7:17], refs[17:24], refs[24]
     copies = [pltpu.make_async_copy(sources[i], held[i], done.at[i]) for i in range(len(sources))]
     large, small = copies[:4], copies[4:]
     for copy in small + large:
@@ -83,7 +88,7 @@
     for copy in small:
         copy.wait()
     x_ref, k_ref, q_ref, dy_ref, rates_ref, residues_ref, filt_ref = held
-    (out_ref, fwd_ref, bwd_ref, hf_ref, hb_ref, aa_ref, bb_ref, g_ref, w_ref,
+    (out_ref, fwd_ref, bwd_ref, hf_ref, aa_ref, bb_ref, g_ref, w_ref,
      e_ref, lanes_ref) = results
 
     def spread(ref):
@@ -128,7 +133,6 @@
         band = pltpu.roll(jnp.broadcast_to(filt, square), 0, 1, stride=1, stride_axis=0)
         high, low = halves(jnp.where(upper, band, 0.0))
         hf_ref[c] = jnp.concatenate([high, low], axis=0)
-        hb_ref[c] = jnp.concatenate([high, low], axis=1)
     share = lax.axis_size("ctx") // filt_ref.shape[0]
     group = lax.axis_index("ctx") // share
     pick = (iota((8, filt_ref.shape[0]), 1) == group).astype(BF16)
@@ -143,7 +147,7 @@
     pack_into(x_ref[...], k_ref[...], q_ref[...], dy_ref[...], out_ref)
 
 
-def main_kernel(in_ref, fwd_ref, bwd_ref, hf_ref, hb_ref, aa_ref, bb_ref, g_ref, w_ref,
+def main_kernel(in_ref, fwd_ref, bwd_ref, hf_ref, aa_ref, bb_ref, g_ref, w_ref,
                 e_ref, lanes_ref, out_ref, sums_ref, in32, out32):
     count = in_ref.shape[0] // IN_ROWS
     rows = OWN * count
@@ -196,7 +200,7 @@
     for c in range(OWN):
         part = slice(c * count, (c + 1) * count)
         z_own.append(z[part] + dot(uu[part], hf_ref[c]))
-        du_own.append(du[part] + dot(dd[part], hb_ref[c], NT))
+        du_own.append(du[part] + fold(dot(d[part], hf_ref[c], NT)))
     put(0, jnp.concatenate(z_own, axis=0))
     du = rounded(jnp.concatenate(du_own, axis=0))
     put(1, du * v)
@@ -291,11 +295,11 @@
     tall2 = (2 * CHUNK, CHUNK)
 
     sources = (x, in_gate, out_gate, out_cot, rates.T, residues.T, mr_filter.T)
-    packed, fwd, bwd, hf, hb, aa, bb, g, w, e, lanes = pl.pallas_call(
+    packed, fwd, bwd, hf, aa, bb, g, w, e, lanes = pl.pallas_call(
         front_kernel,
         out_shape=(
             shape((peers * IN_ROWS, CHUNK), BF16), shape(tall2, BF16), shape(square2, BF16),
-            shape((OWN,) + tall2, BF16), shape((OWN,) + square2, BF16),
+            shape((OWN,) + tall2, BF16),
             shape((2 * CHUNK, 2 * CHUNK), BF16), shape((2 * CHUNK, 2 * CHUNK), BF16),
             shape(tall2, BF16), shape(tall2, BF16),
             shape(square2, BF16), shape((8, LANES), F32),
@@ -312,7 +316,7 @@
         out_shape=(shape((peers * OUT_ROWS, CHUNK), BF16), shape((8, LANES), F32)),
         scratch_shapes=[pltpu.VMEM((peers * IN_ROWS, CHUNK), F32), pltpu.VMEM((peers * OUT_ROWS, CHUNK), F32)],
         compiler_params=ROOM, name="mixer",
-    )(arrived.reshape(peers * IN_ROWS, CHUNK), fwd, bwd, hf, hb, aa, bb, g, w, e, lanes)
+    )(arrived.reshape(peers * IN_ROWS, CHUNK), fwd, bwd, hf, aa, bb, g, w, e, lanes)
 
     returned = lax.all_to_all(back.reshape(peers * OUT_ROWS // 2, 2, CHUNK), "ctx", split_axis=0, concat_axis=0, tiled=True)
 

time: 44.6 us -> 44.6 us (level)
  no operation moved by 1% of the time
where the time goes in v5:
time: 44.6 us; the launch traced here: 44.4 us
  blocking collectives  40.5 us (91%)
  Pallas kernels  3.3 us (7%)
  between operations  0.64 us (1%)
    all_to_all x1, blocking collectives, local(): lax.all_to_all(packed.reshape(3 * peers, OWN, CHUNK), 'ctx', split_axis=0...  23.7 us
    all_to_all x1, blocking collectives, local(): lax.all_to_all(back.reshape(peers * OUT_ROWS // 2, 2, CHUNK), 'ctx', spli...  16.8 us
    pallas_call x1, Pallas kernels, local(): pl.pallas_call(front_kernel, out_shape=(shape((peers * IN_ROWS, CHUNK), B...  1.26 us
    pallas_call x1, Pallas kernels, local(): pl.pallas_call(main_kernel, out_shape=(shape((peers * OUT_ROWS, CHUNK), B...  1.19 us

profile of v5, /device:TPU:1, one launch (start us, length us, event | category | flops | bytes accessed | tf_op | source)
XLA Modules:
  0.0 44.4 jit_solution(14545930286898408817)
XLA Ops:
  0.6 1.3 %front.1 = (bf16[768,128]{1,0:T(8,128)(2,1)S(1)}, bf16[256,128]{1,0:T(8,128)(2,1)S(1)}, bf16[128,256]{1,0:T(8,128)(2,1)S(1)}, bf16[4,256,128]{2,1,0:T(8,128)(2,1...) custom-call(bf16[128,256]{1,0:T(8,128)(2,1)} %refs_0_.1, ...), custom_call_target="tpu_custom_call" | custom-call | tf_op jit(solution)/shard_map/front/pallas_call | solution.py:298
  1.9 23.7 %all_to_all.10 = bf16[192,4,128]{2,1,0:T(4,128)(2,1)S(1)} all-to-all(bf16[192,4,128]{2,1,0:T(4,128)(2,1)S(1)} %bitcast.13), channel_id=1, replica_groups=mesh['ctx'=64,'ch'=4] {'ctx'}, dimensions={0} | all-to-all | bytes 393216 | tf_op jit(solution)/shard_map/all_to_all | solution.py:312
  25.6 1.2 %mixer.1 = (bf16[896,128]{1,0:T(8,128)(2,1)S(1)}, f32[8,128]{1,0:T(8,128)S(1)}) custom-call(bf16[768,128]{1,0:T(8,128)(2,1)S(1)} %bitcast.11, bf16[256,128]{1,0:T(8,128)(2,1)S(1)} %get-tuple-element.25.fwd_ref, bf16[128,256]{1,0:T(8,128)(2,1)S(1)} %get-tuple-element.26.bwd_ref, bf16[4,256,128]{2,1,0:T(8,128)(2,1)S(1)} %get-tuple-element.27.hf_ref, ...), custom_call_target="tpu_custom_call" | custom-call | tf_op jit(solution)/shard_map/mixer/pallas_call | solution.py:314
  26.8 0.0 copy-start
  26.8 16.8 %all_to_all.11 = bf16[448,2,128]{2,1,0:T(2,128)(2,1)S(1)} all-to-all(bf16[448,2,128]{2,1,0:T(2,128)(2,1)S(1)} %bitcast.12), channel_id=1, replica_groups=mesh['ctx'=64,'ch'=4] {'ctx'}, dimensions={0} | all-to-all | bytes 458752 | tf_op jit(solution)/shard_map/all_to_all | solution.py:321
  43.6 0.0 copy-done
  43.6 0.8 %unpack.1 = (bf16[128,256]{1,0:T(8,128)(2,1)}, bf16[128,256]{1,0:T(8,128)(2,1)}, bf16[128,256]{1,0:T(8,128)(2,1)}, f32[16,128]{1,0:T(8,128)}, f32[4,16]{1,0:T(4,128)}, /*index=5*/f32[4,16]{1,0:T(4,128)}) custom-call(bf16[896,128]{1,0:T(8,128)(2,1)S(1)} %bitcast.10, bf16[128,256]{1,0:T(8,128)(2,1)S(1)} %copy-done, f32[8,128]{1,0:T(8,128)S(1)} %get-tuple-element.35.refs_2_, ...), custom_call_target="tpu_custom_call" | custom-call | tf_op jit(solution)/shard_map/unpack/pallas_call | solution.py:323
Async XLA Ops:
  26.8 16.8 %copy-start = (bf16[128,256]{1,0:T(8,128)(2,1)S(1)}, bf16[128,256]{1,0:T(8,128)(2,1)}, u32[]{:S(2)}) copy-start(bf16[128,256]{1,0:T(8,128)(2,1)} %refs_1_.3) | copy-start | bytes 196612

commit v6 on v3

--- a/solution.py
+++ b/solution.py
@@ -104,7 +104,7 @@
     lanes_ref[1:2, :] = jnp.sum(jnp.where(diagonal, residues, 0.0), axis=0, keepdims=True)
     lanes_ref[2:8, :] = jnp.zeros((6, LANES), F32)
     decay = jnp.exp(-rates * step)
-    after = jnp.exp(-rates * (step + 1.0))
+    after = decay * jnp.exp(-rates)
     before = jnp.exp(-rates * (CHUNK - 1.0 - step))
     high, low = halves(jnp.concatenate([decay, decay * step], axis=0))
     e_ref[...] = jnp.concatenate([high, low], axis=1)
@@ -185,9 +185,9 @@
 
     def states(value):
         high = rounded(value)
-        both = jnp.where(iota(value.shape, 1) < LANES // 2, high, value - high)
-        parts = [jnp.where(own_lanes(value.shape, c), both, 0.0) for c in range(OWN)]
-        stacked = jnp.concatenate(parts, axis=0).astype(BF16)
+        both = jnp.where(iota(value.shape, 1) < LANES // 2, high, value - high).astype(BF16)
+        none = jnp.zeros_like(both)
+        stacked = jnp.concatenate([jnp.where(own_lanes(value.shape, c), both, none) for c in range(OWN)], axis=0)
         return jnp.concatenate([stacked, stacked], axis=1)
 
     z = dot(states(ahead), g_ref[...])

time: 44.6 us -> 44.6 us (level)
  no operation moved by 1% of the time
where the time goes in v6:
time: 44.6 us; the launch traced here: 44.4 us
  blocking collectives  40.5 us (91%)
  Pallas kernels  3.3 us (7%)
  between operations  0.64 us (1%)
    all_to_all x1, blocking collectives, local(): lax.all_to_all(packed.reshape(3 * peers, OWN, CHUNK), 'ctx', split_axis=0...  23.7 us
    all_to_all x1, blocking collectives, local(): lax.all_to_all(back.reshape(peers * OUT_ROWS // 2, 2, CHUNK), 'ctx', spli...  16.8 us
    pallas_call x1, Pallas kernels, local(): pl.pallas_call(front_kernel, out_shape=(shape((peers * IN_ROWS, CHUNK), B...  1.26 us
    pallas_call x1, Pallas kernels, local(): pl.pallas_call(main_kernel, out_shape=(shape((peers * OUT_ROWS, CHUNK), B...  1.19 us

profile of v6, /device:TPU:1, one launch (start us, length us, event | category | flops | bytes accessed | tf_op | source)
XLA Modules:
  0.0 44.4 jit_solution(5824403933760619468)
XLA Ops:
  0.6 1.3 %front.1 = (bf16[768,128]{1,0:T(8,128)(2,1)S(1)}, bf16[256,128]{1,0:T(8,128)(2,1)S(1)}, bf16[128,256]{1,0:T(8,128)(2,1)S(1)}, bf16[4,256,128]{2,1,0:T(8,128)(2,1...) custom-call(bf16[128,256]{1,0:T(8,128)(2,1)} %refs_0_.1, ...), custom_call_target="tpu_custom_call" | custom-call | tf_op jit(solution)/shard_map/front/pallas_call | solution.py:294
  1.9 23.7 %all_to_all.10 = bf16[192,4,128]{2,1,0:T(4,128)(2,1)S(1)} all-to-all(bf16[192,4,128]{2,1,0:T(4,128)(2,1)S(1)} %bitcast.13), channel_id=1, replica_groups=mesh['ctx'=64,'ch'=4] {'ctx'}, dimensions={0} | all-to-all | bytes 393216 | tf_op jit(solution)/shard_map/all_to_all | solution.py:308
  25.6 1.2 %mixer.1 = (bf16[896,128]{1,0:T(8,128)(2,1)S(1)}, f32[8,128]{1,0:T(8,128)S(1)}) custom-call(bf16[768,128]{1,0:T(8,128)(2,1)S(1)} %bitcast.11, bf16[256,128]{1,0:T(8,128)(2,1)S(1)} %get-tuple-element.26.fwd_ref, bf16[128,256]{1,0:T(8,128)(2,1)S(1)} %get-tuple-element.27.bwd_ref, bf16[4,256,128]{2,1,0:T(8,128)(2,1)S(1)} %get-tuple-element.28.hf_ref, ...), custom_call_target="tpu_custom_call" | custom-call | tf_op jit(solution)/shard_map/mixer/pallas_call | solution.py:310
  26.8 0.0 copy-start
  26.8 16.8 %all_to_all.11 = bf16[448,2,128]{2,1,0:T(2,128)(2,1)S(1)} all-to-all(bf16[448,2,128]{2,1,0:T(2,128)(2,1)S(1)} %bitcast.12), channel_id=1, replica_groups=mesh['ctx'=64,'ch'=4] {'ctx'}, dimensions={0} | all-to-all | bytes 458752 | tf_op jit(solution)/shard_map/all_to_all | solution.py:317
  43.6 0.0 copy-done
  43.6 0.8 %unpack.1 = (bf16[128,256]{1,0:T(8,128)(2,1)}, bf16[128,256]{1,0:T(8,128)(2,1)}, bf16[128,256]{1,0:T(8,128)(2,1)}, f32[16,128]{1,0:T(8,128)}, f32[4,16]{1,0:T(4,128)}, /*index=5*/f32[4,16]{1,0:T(4,128)}) custom-call(bf16[896,128]{1,0:T(8,128)(2,1)S(1)} %bitcast.10, bf16[128,256]{1,0:T(8,128)(2,1)S(1)} %copy-done, f32[8,128]{1,0:T(8,128)S(1)} %get-tuple-element.37.refs_2_, ...), custom_call_target="tpu_custom_call" | custom-call | tf_op jit(solution)/shard_map/unpack/pallas_call | solution.py:319
Async XLA Ops:
  26.8 16.8 %copy-start = (bf16[128,256]{1,0:T(8,128)(2,1)S(1)}, bf16[128,256]{1,0:T(8,128)(2,1)}, u32[]{:S(2)}) copy-start(bf16[128,256]{1,0:T(8,128)(2,1)} %refs_1_.3) | copy-start | bytes 196612

commit v7 on v3

--- a/solution.py
+++ b/solution.py
@@ -205,8 +205,8 @@
     dv = dv.astype(BF16)
     dvv = jnp.concatenate([dv, dv_next.astype(BF16)], axis=1)
     put(2, dot(dvv, bwd_ref[...], NT))
-    cross = dot(dv, jnp.concatenate([mirrored(xx[:, :CHUNK]), mirrored(xx[:, CHUNK:])], axis=1), TN)
-    sums = diagonal_sums(jnp.where(causal((CHUNK, CHUNK)), cross[:, :CHUNK], cross[:, CHUNK:]))
+    cross = dot(jnp.concatenate([mirrored(xx[:, :CHUNK]), mirrored(xx[:, CHUNK:])], axis=1), dv, TN)
+    sums = diagonal_sums(jnp.where(causal((CHUNK, CHUNK)), cross[:CHUNK], cross[CHUNK:]))
     high = rounded(sums)
     out32[pl.ds(3 * OWN, count, stride=OUT_ROWS), :] = jnp.broadcast_to(high, (count, CHUNK))
     out32[pl.ds(3 * OWN + 1, count, stride=OUT_ROWS), :] = jnp.broadcast_to(sums - high, (count, CHUNK))

time: 44.6 us -> 44.7 us (level)
  no operation moved by 1% of the time
where the time goes in v7:
time: 44.7 us; the launch traced here: 44.4 us
  blocking collectives  40.5 us (91%)
  Pallas kernels  3.31 us (7%)
  between operations  0.64 us (1%)
    all_to_all x1, blocking collectives, local(): lax.all_to_all(packed.reshape(3 * peers, OWN, CHUNK), 'ctx', split_axis=0...  23.7 us
    all_to_all x1, blocking collectives, local(): lax.all_to_all(back.reshape(peers * OUT_ROWS // 2, 2, CHUNK), 'ctx', spli...  16.8 us
    pallas_call x1, Pallas kernels, local(): pl.pallas_call(front_kernel, out_shape=(shape((peers * IN_ROWS, CHUNK), B...  1.26 us
    pallas_call x1, Pallas kernels, local(): pl.pallas_call(main_kernel, out_shape=(shape((peers * OUT_ROWS, CHUNK), B...  1.2 us

profile of v7, /device:TPU:1, one launch (start us, length us, event | category | flops | bytes accessed | tf_op | source)
XLA Modules:
  0.0 44.4 jit_solution(12562554718524297767)
XLA Ops:
  0.6 1.3 %front.1 = (bf16[768,128]{1,0:T(8,128)(2,1)S(1)}, bf16[256,128]{1,0:T(8,128)(2,1)S(1)}, bf16[128,256]{1,0:T(8,128)(2,1)S(1)}, bf16[4,256,128]{2,1,0:T(8,128)(2,1...) custom-call(bf16[128,256]{1,0:T(8,128)(2,1)} %refs_0_.1, ...), custom_call_target="tpu_custom_call" | custom-call | tf_op jit(solution)/shard_map/front/pallas_call | solution.py:294
  1.9 23.7 %all_to_all.10 = bf16[192,4,128]{2,1,0:T(4,128)(2,1)S(1)} all-to-all(bf16[192,4,128]{2,1,0:T(4,128)(2,1)S(1)} %bitcast.13), channel_id=1, replica_groups=mesh['ctx'=64,'ch'=4] {'ctx'}, dimensions={0} | all-to-all | bytes 393216 | tf_op jit(solution)/shard_map/all_to_all | solution.py:308
  25.6 1.2 %mixer.1 = (bf16[896,128]{1,0:T(8,128)(2,1)S(1)}, f32[8,128]{1,0:T(8,128)S(1)}) custom-call(bf16[768,128]{1,0:T(8,128)(2,1)S(1)} %bitcast.11, bf16[256,128]{1,0:T(8,128)(2,1)S(1)} %get-tuple-element.26.fwd_ref, bf16[128,256]{1,0:T(8,128)(2,1)S(1)} %get-tuple-element.27.bwd_ref, bf16[4,256,128]{2,1,0:T(8,128)(2,1)S(1)} %get-tuple-element.28.hf_ref, ...), custom_call_target="tpu_custom_call" | custom-call | tf_op jit(solution)/shard_map/mixer/pallas_call | solution.py:310
  26.8 0.0 copy-start
  26.8 16.8 %all_to_all.11 = bf16[448,2,128]{2,1,0:T(2,128)(2,1)S(1)} all-to-all(bf16[448,2,128]{2,1,0:T(2,128)(2,1)S(1)} %bitcast.12), channel_id=1, replica_groups=mesh['ctx'=64,'ch'=4] {'ctx'}, dimensions={0} | all-to-all | bytes 458752 | tf_op jit(solution)/shard_map/all_to_all | solution.py:317
  43.6 0.0 copy-done
  43.6 0.8 %unpack.1 = (bf16[128,256]{1,0:T(8,128)(2,1)}, bf16[128,256]{1,0:T(8,128)(2,1)}, bf16[128,256]{1,0:T(8,128)(2,1)}, f32[16,128]{1,0:T(8,128)}, f32[4,16]{1,0:T(4,128)}, /*index=5*/f32[4,16]{1,0:T(4,128)}) custom-call(bf16[896,128]{1,0:T(8,128)(2,1)S(1)} %bitcast.10, bf16[128,256]{1,0:T(8,128)(2,1)S(1)} %copy-done, f32[8,128]{1,0:T(8,128)S(1)} %get-tuple-element.37.refs_2_, ...), custom_call_target="tpu_custom_call" | custom-call | tf_op jit(solution)/shard_map/unpack/pallas_call | solution.py:319
Async XLA Ops:
  26.8 16.8 %copy-start = (bf16[128,256]{1,0:T(8,128)(2,1)S(1)}, bf16[128,256]{1,0:T(8,128)(2,1)}, u32[]{:S(2)}) copy-start(bf16[128,256]{1,0:T(8,128)(2,1)} %refs_1_.3) | copy-start | bytes 196612
